TPU v7x, 512 devices: a whole 4x8x8 slice. The times are simulated.
512 devices in a mesh: row: 8 (over z_lo, core), col: 8 (over x, z_hi), tm: 8 (over y).
Axes of the slice: x: 4, y: 8, z: 8 (z_hi: 2, z_lo: 4; z = z_hi * 4 + z_lo), core: 2. Of those that a mesh axis runs over, the one named last changes fastest.
Arguments:
- green_occ: bfloat16 [16, 256, 30720], P('tm', 'row', 'col'), may hold values from -6 to 6
- green_virt: bfloat16 [16, 256, 30720], P('tm', 'row', 'col'), may hold values from -6 to 6
- adjoint_w: bfloat16 [16, 256, 30720], P(None, 'row', ('col', 'tm')), may hold values from -6 to 6
- grad_basis: float32 [3, 256], P(None, 'row'), may hold values from -6 to 6
- owner_map: int32 [30720], replicated, may hold values from 0 to 999
- block_offset: int32 [8], P('row'), may hold values from 0 to 30688
Outputs:
- chi_freq: bfloat16 [16, 256, 30720], P(None, 'row', ('col', 'tm'))
- forces: float32 [3, 1000], replicated
All inputs are finite; a program needn't handle non-finite values.
Results may differ from a plain program's by a relative error of at most 0.0085.
Values may be sent and summed in bfloat16 or wider, within the bound.
No kernel may reach another device: no remote copies, remote signals or barrier semaphores. Data moves between devices by JAX's collectives and lax.ppermute only.
A program may use at most 64 MiB of HBM per device.

v0:
```python
import math

import jax
import jax.numpy as jnp
from jax import lax
from jax.sharding import PartitionSpec as P

NG = 30720
NTAU = 16
NATOM = 1000


def cos_table(count):
    steps = jnp.arange(count).astype(jnp.float32)
    tau = 0.1 * jnp.power(jnp.float32(1.35), steps)
    omega = 0.15 * jnp.power(jnp.float32(1.35), steps)
    return jnp.cos(omega[:, None] * tau[None, :]) / 4.0


def on_device(green_occ, green_virt, adjoint_w, grad_basis, owner_map, block_offset):
    table = cos_table(NTAU)
    scale = 1.0 / math.sqrt(NTAU * NG)
    row_count = green_occ.shape[1]
    product = (green_occ.astype(jnp.float32) * green_virt.astype(jnp.float32)).astype(jnp.bfloat16)
    chi_freq = jnp.einsum(
        "kt,tnc->knc",
        table,
        lax.all_to_all(product, "tm", split_axis=2, concat_axis=0, tiled=True).astype(jnp.float32),
        precision=lax.Precision.HIGHEST,
    ).astype(jnp.bfloat16)
    partial_value = (
        jnp.sum(adjoint_w.astype(jnp.float32) * chi_freq.astype(jnp.float32), axis=(0, 2)) * scale
    )
    owners = lax.dynamic_slice_in_dim(owner_map, block_offset[0], row_count, 0)
    onehot = (owners[:, None] == jnp.arange(NATOM)[None, :]).astype(jnp.float32)
    energy = lax.psum(partial_value, ("col", "tm"))
    local_forces = jnp.dot(
        grad_basis * energy[None, :],
        onehot,
        precision=lax.Precision.HIGHEST,
        preferred_element_type=jnp.float32,
    )
    forces = lax.psum(local_forces, "row")
    return (chi_freq, forces)


def solution(mesh):
    in_specs = (
        P("tm", "row", "col"),
        P("tm", "row", "col"),
        P(None, "row", ("col", "tm")),
        P(None, "row"),
        P(),
        P("row"),
    )
    out_specs = (P(None, "row", ("col", "tm")), P())
    return jax.shard_map(
        on_device, mesh=mesh, in_specs=in_specs, out_specs=out_specs, check_vma=False
    )
```

profile of v0, /device:TPU:1, one launch (start us, length us, event | category | flops | bytes accessed | tf_op | source)
XLA Modules:
  0.0 282.4 jit_solution(8296169190990714850)
XLA Ops:
  0.6 1.3 multiply_convert_fusion
  1.9 1.4 copy.16
  3.3 2.5 reshape.19
  5.9 7.7 %all-to-all-start = ((bf16[8,2,15360]{2,1,0:T(2,128)(2,1)}), bf16[8,2,15360]{2,1,0:T(2,128)(2,1)S(1)}, u32[]{:S(2)}, u32[]{:S(2)}) async-start(bf16[8,2,15360]{2,1,0:T(2,128)(2,1)} %reshape.19), calls=%async_computation | async-start | bytes 983040 | tf_op jit(solution)/shard_map/all_to_all | solution.py:28
  14.2 0.8 dynamic_slice.3
  15.0 12.4 %all-to-all-done = bf16[8,2,15360]{2,1,0:T(2,128)(2,1)S(1)} async-done(((bf16[8,2,15360]{2,1,0:T(2,128)(2,1)}), bf16[8,2,15360]{2,1,0:T(2,128)(2,1)S(1)}, u32[]{:S(2)}, u32[]{:S(2)}) %all-to-all-start) | async-done | bytes 491552 | tf_op jit(solution)/shard_map/all_to_all | solution.py:28
  27.4 1.0 reshape.20
  28.4 0.0 copy-start
  28.4 1.5 copy.17
  29.9 0.0 copy-start.1
  29.9 0.4 all_to_all.16
  30.3 0.0 copy-done
  30.4 1.1 multiply_reduce_fusion
  31.5 1.1 copy.19
  32.5 196.4 %psum.14 = f32[32]{0:T(128)S(1)} all-reduce(f32[32]{0:T(128)S(1)} %broadcast_multiply_fusion), channel_id=1, replica_groups=mesh['row'=8,'col'=8,'tm'=8] {'col','tm'}, use_global_device_ids=true, to_apply=%region_1.0 | all-reduce | flops 32 | bytes 256 | tf_op jit(solution)/shard_map/psum | solution.py:36
  228.9 0.0 copy-done.1
  228.9 0.2 fusion
  229.1 53.3 %psum.15 = f32[3,1000]{1,0:T(4,128)} all-reduce(f32[3,1000]{1,0:T(4,128)S(1)} %fusion), channel_id=1, replica_groups=mesh['row'=8,'col'=8,'tm'=8] {'row'}, use_global_device_ids=true, to_apply=%region_2.0 | all-reduce | flops 3000 | bytes 24000 | tf_op jit(solution)/shard_map/psum | solution.py:43
  (2 shorter events, 0.0 us)
Async XLA Ops:
  5.9 21.5 %all-to-all-start = ((bf16[8,2,15360]{2,1,0:T(2,128)(2,1)}), bf16[8,2,15360]{2,1,0:T(2,128)(2,1)S(1)}, u32[]{:S(2)}, u32[]{:S(2)}) async-start(bf16[8,2,15360]{2,1,0:T(2,128)(2,1)} %reshape.19), calls=%async_computation | async-start | bytes 983040 | tf_op jit(solution)/shard_map/all_to_all | solution.py:28
  28.4 2.0 copy-start
  29.9 199.0 %copy-start.1 = (f32[3,32]{1,0:T(4,128)S(1)}, f32[3,32]{1,0:T(4,128)}, u32[]{:S(2)}) copy-start(f32[3,32]{1,0:T(4,128)} %param.9) | copy-start | bytes 1156
where the time goes:
time: 283 us; the launch traced here: 282 us
  blocking collectives  250 us (88%)
  waiting for transfers between devices  12.4 us (4%)
  local copies, waits for them, and re-layouts  8.71 us (3%)
  starting transfers between devices  7.65 us (3%)
    psum x1, blocking collectives, on_device(): energy = lax.psum(partial_value, ('col', 'tm'))  196 us
    psum x1, blocking collectives, on_device(): forces = lax.psum(local_forces, 'row')  53.3 us
    all_to_all x1, waiting for transfers between devices, on_device(): lax.all_to_all(product, 'tm', split_axis=2, concat_axis=0, tiled=True)  12.4 us
    all_to_all x1, starting transfers between devices, on_device(): lax.all_to_all(product, 'tm', split_axis=2, concat_axis=0, tiled=True)  7.65 us
  transfers between devices with their start and end apart: 1, of which 1 were waited for; matrix products, arithmetic and copies ran while one was open for 0% of the time, Pallas kernels for 0%

commit v1 on v0

v1 whole, which is shorter than its diff:
```python
import functools
import math

import jax
import jax.numpy as jnp
import ml_dtypes
import numpy as np
from jax import lax
from jax.experimental import pallas as pl
from jax.experimental.pallas import tpu as pltpu
from jax.sharding import PartitionSpec as P

NG = 30720
NTAU = 16
NATOM = 1000
GROUP = 16
LANES = 128


def transform_matrix():
    steps = np.arange(NTAU, dtype=np.float64)
    tau = 0.1 * 1.35**steps
    omega = 0.15 * 1.35**steps
    table = np.cos(omega[:, None] * tau[None, :]) / 4.0
    high = table.astype(ml_dtypes.bfloat16)
    low = (table - high.astype(np.float64)).astype(ml_dtypes.bfloat16)
    eye = np.eye(GROUP)
    return [np.kron(part.astype(np.float64), eye).astype(ml_dtypes.bfloat16) for part in (high, low)]


def product_kernel(n_dest, occ_ref, virt_ref, out_ref):
    width = out_ref.shape[-1]
    product = occ_ref[0].astype(jnp.float32) * virt_ref[0].astype(jnp.float32)
    for j in range(n_dest):
        out_ref[j, 0] = product[:, j * width : (j + 1) * width].astype(jnp.bfloat16)


def transform_kernel(n_copies, high_ref, low_ref, prod_ref, adj_ref, chi_ref, energy_ref):
    n_freq, rows, width = chi_ref.shape
    total = jnp.zeros((1, LANES), jnp.float32)
    for start in range(0, rows, GROUP):
        block = pl.ds(start, GROUP)
        times = prod_ref[:, block, :].reshape(NTAU * GROUP, width)
        chi = jnp.dot(high_ref[...], times, preferred_element_type=jnp.float32)
        chi += jnp.dot(low_ref[...], times, preferred_element_type=jnp.float32)
        chi = chi.reshape(n_freq, GROUP, width).astype(jnp.bfloat16)
        chi_ref[:, block, :] = chi
        terms = adj_ref[:, block, :].astype(jnp.float32) * chi.astype(jnp.float32)
        energy = jnp.sum(jnp.sum(terms, axis=0), axis=1, keepdims=True)
        row = lax.broadcasted_iota(jnp.int32, (GROUP, LANES), 0) + start
        lane = lax.broadcasted_iota(jnp.int32, (GROUP, LANES), 1)
        spread = jnp.where(lane % rows == row, energy, 0.0)
        total += jnp.sum(spread, axis=0, keepdims=True)
    energy_ref[...] = jnp.broadcast_to(total, (n_copies, LANES))


def forces_kernel(rows, message_ref, forces_ref):
    n_block = message_ref.shape[0]
    messages = message_ref[...]
    weighted = jnp.sum(messages, axis=1)
    first = messages[:, 0, :]

    def along_lanes(values, part):
        return jnp.concatenate(
            [values[i : i + 1, part * rows : (part + 1) * rows] for i in range(n_block)], axis=1
        )

    weights = jnp.concatenate([along_lanes(weighted, part) for part in range(3)], axis=0)
    owners = along_lanes(first, 3).astype(jnp.int32)
    atoms = lax.broadcasted_iota(jnp.int32, (NATOM, owners.shape[1]), 0)
    onehot = jnp.where(atoms == owners, 1.0, 0.0).astype(jnp.bfloat16)
    rest = weights
    forces = jnp.zeros((3, NATOM), jnp.float32)
    for _ in range(3):
        part = rest.astype(jnp.bfloat16)
        rest = rest - part.astype(jnp.float32)
        forces += lax.dot_general(
            part, onehot, (((1,), (1,)), ((), ())), preferred_element_type=jnp.float32
        )
    forces_ref[...] = forces


def on_device(sizes, green_occ, green_virt, adjoint_w, grad_basis, owner_map, block_offset):
    n_row, n_col, n_tm = sizes
    n_time, rows, columns = green_occ.shape
    width = columns // n_tm
    scale = 1.0 / math.sqrt(NTAU * NG)
    high, low = transform_matrix()

    product = pl.pallas_call(
        functools.partial(product_kernel, n_tm),
        grid=(n_time,),
        in_specs=[pl.BlockSpec((1, rows, columns), lambda t: (t, 0, 0))] * 2,
        out_specs=pl.BlockSpec((n_tm, 1, rows, width), lambda t: (0, t, 0, 0)),
        out_shape=jax.ShapeDtypeStruct((n_tm, n_time, rows, width), jnp.bfloat16),
        name="product",
    )(green_occ, green_virt)
    times = lax.all_to_all(product, "tm", split_axis=0, concat_axis=0, tiled=True)
    times = times.reshape(NTAU, rows, width)

    owners = lax.dynamic_slice_in_dim(owner_map, block_offset[0], rows, 0)
    weight = jnp.concatenate([grad_basis.reshape(3 * rows) * scale, jnp.zeros((rows,), jnp.float32)])
    label = jnp.concatenate([jnp.zeros((3 * rows,), jnp.float32), owners.astype(jnp.float32)])

    chi_freq, energy = pl.pallas_call(
        functools.partial(transform_kernel, n_tm),
        out_shape=(
            jax.ShapeDtypeStruct((NTAU, rows, width), jnp.bfloat16),
            jax.ShapeDtypeStruct((n_tm, LANES), jnp.float32),
        ),
        compiler_params=pltpu.CompilerParams(vmem_limit_bytes=32 << 20),
        name="transform",
    )(jnp.asarray(high), jnp.asarray(low), times, adjoint_w)

    energy = lax.all_to_all(energy, "tm", split_axis=0, concat_axis=0, tiled=True)
    message = jnp.sum(energy, axis=0) * weight + label
    message = jnp.broadcast_to(message[None, :], (n_row * n_col, LANES))
    message = lax.all_to_all(message, ("row", "col"), split_axis=0, concat_axis=0, tiled=True)
    forces = pl.pallas_call(
        functools.partial(forces_kernel, rows),
        out_shape=jax.ShapeDtypeStruct((3, NATOM), jnp.float32),
        compiler_params=pltpu.CompilerParams(vmem_limit_bytes=32 << 20),
        name="forces",
    )(message.reshape(n_row, n_col, LANES))
    return (chi_freq, forces)


def solution(mesh):
    in_specs = (
        P("tm", "row", "col"),
        P("tm", "row", "col"),
        P(None, "row", ("col", "tm")),
        P(None, "row"),
        P(),
        P("row"),
    )
    out_specs = (P(None, "row", ("col", "tm")), P())
    sizes = tuple(mesh.shape[name] for name in ("row", "col", "tm"))
    return jax.shard_map(
        functools.partial(on_device, sizes),
        mesh=mesh,
        in_specs=in_specs,
        out_specs=out_specs,
        check_vma=False,
    )
```

time: 283 us -> 65.2 us (0.23)
  blocking collectives: 250 us -> 27.1 us
  local copies, waits for them, and re-layouts: 8.71 us -> 0.79 us
  waiting for transfers between devices: 12.4 us -> 19 us
  Pallas kernels: 0 us -> 4.63 us
  starting transfers between devices: 7.65 us -> 11.1 us
    psum x2 -> x0, blocking collectives: 250 us -> none  [the longest x1 196 us: on_device(): energy = lax.psum(partial_value, ('col', 'tm'))]
    all_to_all x0 -> x1, blocking collectives: none -> 27.1 us  [on_device(): lax.all_to_all(message, ('row', 'col'), split_axis=0, concat_axis=0, tile...]
    all_to_all x1 -> x2, waiting for transfers between devices: 12.4 us -> 19 us  [the longest x1 13.4 us: on_device(): lax.all_to_all(product, 'tm', split_axis=0, concat_axis=0, tiled=True)]
    pallas_call x0 -> x3, Pallas kernels: none -> 4.63 us  [the longest x1 2.17 us: on_device(): pl.pallas_call(functools.partial(product_kernel, n_tm), grid=(n_time,), i...]
    unnamed x7 -> x8, local copies, waits for them, and re-layouts: 4.61 us -> 0.69 us
    all_to_all x1 -> x2, starting transfers between devices: 7.65 us -> 11.1 us  [the longest x1 7.79 us: on_device(): lax.all_to_all(product, 'tm', split_axis=0, concat_axis=0, tiled=True)]
  transfers between devices with their start and end apart: 1 -> 2, of which waited for: 1 -> 2; matrix products, arithmetic and copies ran while one was open for 0% -> 1% of each run, Pallas kernels for 0% -> 0%
where the time goes in v1:
time: 65.2 us; the launch traced here: 64.9 us
  blocking collectives  27.1 us (42%)
  waiting for transfers between devices  19 us (29%)
  starting transfers between devices  11.1 us (17%)
  Pallas kernels  4.63 us (7%)
  between operations  1.31 us (2%)
  other arithmetic  0.88 us (1%)
  local copies, waits for them, and re-layouts  0.79 us (1%)
    all_to_all x1, blocking collectives, on_device(): lax.all_to_all(message, ('row', 'col'), split_axis=0, concat_axis=0, tile...  27.1 us
    all_to_all x1, waiting for transfers between devices, on_device(): lax.all_to_all(product, 'tm', split_axis=0, concat_axis=0, tiled=True)  13.4 us
    all_to_all x1, starting transfers between devices, on_device(): lax.all_to_all(product, 'tm', split_axis=0, concat_axis=0, tiled=True)  7.79 us
    all_to_all x1, waiting for transfers between devices, on_device(): lax.all_to_all(energy, 'tm', split_axis=0, concat_axis=0, tiled=True)  5.6 us
    all_to_all x1, starting transfers between devices, on_device(): lax.all_to_all(energy, 'tm', split_axis=0, concat_axis=0, tiled=True)  3.34 us
    pallas_call x1, Pallas kernels, on_device(): pl.pallas_call(functools.partial(product_kernel, n_tm), grid=(n_time,), i...  2.17 us
  transfers between devices with their start and end apart: 2, of which 2 were waited for; matrix products, arithmetic and copies ran while one was open for 1% of the time, Pallas kernels for 0%

profile of v1, /device:TPU:1, one launch (start us, length us, event | category | flops | bytes accessed | tf_op | source)
XLA Modules:
  0.0 64.9 jit_solution(14023786174382842695)
XLA Ops:
  0.6 2.2 %product.1 = bf16[8,2,32,480]{3,2,1,0:T(8,128)(2,1)} custom-call(bf16[2,32,3840]{2,1,0:T(8,128)(2,1)} %occ_ref.1, bf16[2,32,3840]{2,1,0:T(8,128)(2,1)} %virt_ref.1), custom_call_target="tpu_custom_call" | custom-call | tf_op jit(solution)/shard_map/product/pallas_call | solution.py:90
  2.8 0.0 copy-start
  2.8 0.0 copy-start.1
  2.8 0.0 copy-start.2
  2.8 7.8 %all-to-all-start = ((bf16[8,2,32,480]{3,2,1,0:T(8,128)(2,1)}), bf16[8,2,32,480]{3,2,1,0:T(8,128)(2,1)S(1)}, u32[]{:S(2)}, u32[]{:S(2)}) async-start(bf16[8,2,32,480]{3,2,1,0:T(8,128)(2,1)} %product.1), calls=%async_computation | async-start | bytes 1048576 | tf_op jit(solution)/shard_map/all_to_all | solution.py:98
  11.3 0.0 copy-start.3
  11.3 0.7 %copy-done.3 = f32[3,32]{1,0:T(4,128)S(1)} copy-done((f32[3,32]{1,0:T(4,128)S(1)}, f32[3,32]{1,0:T(4,128)}, u32[]{:S(2)}) %copy-start.3) | copy-done | bytes 408
  11.9 13.4 %all-to-all-done = bf16[8,2,32,480]{3,2,1,0:T(8,128)(2,1)S(1)} async-done(((bf16[8,2,32,480]{3,2,1,0:T(8,128)(2,1)}), bf16[8,2,32,480]{3,2,1,0:T(8,128)(2,1)S(1)}, u32[]{:S(2)}, u32[]{:S(2)}) %all-to-all-start) | async-done | bytes 491552 | tf_op jit(solution)/shard_map/all_to_all | solution.py:98
  25.4 0.0 copy-done
  25.4 0.0 copy-done.1
  25.4 0.0 copy-done.2
  25.4 1.3 %transform.1 = (bf16[16,32,480]{2,1,0:T(8,128)(2,1)}, f32[8,128]{1,0:T(8,128)}) custom-call(bf16[256,256]{1,0:T(8,128)(2,1)S(1)} %copy-done.1, bf16[256,256]{1,0:T(8,128)(2,1)S(1)} %copy-done.2, bf16[16,32,480]{2,1,0:T(8,128)(2,1)S(1)} %bitcast.9, bf16[16,32,480]{2,1,0:T(8,128)(2,1)S(1)} %copy-done), custom_call_target="tpu_custom_call" | custom-call | tf_op jit(solution)/shard_map/transform/pallas_call | solution.py:105
  26.6 3.3 %all-to-all-start.1 = ((f32[8,1,128]{2,1,0:T(1,128)}), f32[8,1,128]{2,1,0:T(1,128)S(1)}, u32[]{:S(2)}, u32[]{:S(2)}) async-start(f32[8,1,128]{2,1,0:T(1,128)} %bitcast.2), calls=%async_computation.1 | async-start | bytes 8192 | tf_op jit(solution)/shard_map/all_to_all | solution.py:115
  30.0 0.8 %dynamic-slice_convert_fusion = f32[32]{0:T(128)S(1)} fusion(s32[30720]{0:T(1024)} %param.12, s32[]{:T(128)S(6)} %select_n.3), kind=kLoop, calls=%fused_computation.2 | loop fusion | flops 32 | bytes 260 | tf_op jit(solution)/shard_map/convert_element_type | solution.py:103
  30.7 0.1 mul.14
  30.8 5.6 %all-to-all-done.1 = f32[8,1,128]{2,1,0:T(1,128)S(1)} async-done(((f32[8,1,128]{2,1,0:T(1,128)}), f32[8,1,128]{2,1,0:T(1,128)S(1)}, u32[]{:S(2)}, u32[]{:S(2)}) %all-to-all-start.1) | async-done | bytes 4128 | tf_op jit(solution)/shard_map/all_to_all | solution.py:115
  36.4 0.1 pad_add_fusion
  36.5 27.1 %all_to_all.20 = f32[64,1,128]{2,1,0:T(1,128)S(1)} all-to-all(f32[64,1,128]{2,1,0:T(1,128)S(1)} %broadcast_in_dim.2), channel_id=1, replica_groups=mesh['row'=8,'col'=8,'tm'=8] {'row','col'}, dimensions={0} | all-to-all | bytes 65536 | tf_op jit(solution)/shard_map/all_to_all | solution.py:118
  63.6 1.2 %forces.1 = f32[3,1000]{1,0:T(4,128)} custom-call(f32[8,8,128]{2,1,0:T(8,128)S(1)} %bitcast.10), custom_call_target="tpu_custom_call" | custom-call | tf_op jit(solution)/shard_map/forces/pallas_call | solution.py:119
  (3 shorter events, 0.1 us)
Async XLA Ops:
  2.8 22.6 %copy-start = (bf16[16,32,480]{2,1,0:T(8,128)(2,1)S(1)}, bf16[16,32,480]{2,1,0:T(8,128)(2,1)}, u32[]{:S(2)}) copy-start(bf16[16,32,480]{2,1,0:T(8,128)(2,1)} %adj_ref.1) | copy-start | bytes 1474564
  2.8 22.6 %copy-start.1 = (bf16[256,256]{1,0:T(8,128)(2,1)S(1)}, bf16[256,256]{1,0:T(8,128)(2,1)}, u32[]{:S(2)}) copy-start(bf16[256,256]{1,0:T(8,128)(2,1)} %constant.4.clone.high_ref) | copy-start | bytes 393220
  2.8 22.6 %copy-start.2 = (bf16[256,256]{1,0:T(8,128)(2,1)S(1)}, bf16[256,256]{1,0:T(8,128)(2,1)}, u32[]{:S(2)}) copy-start(bf16[256,256]{1,0:T(8,128)(2,1)} %constant.5.clone.low_ref) | copy-start | bytes 393220
  2.8 22.5 %all-to-all-start = ((bf16[8,2,32,480]{3,2,1,0:T(8,128)(2,1)}), bf16[8,2,32,480]{3,2,1,0:T(8,128)(2,1)S(1)}, u32[]{:S(2)}, u32[]{:S(2)}) async-start(bf16[8,2,32,480]{3,2,1,0:T(8,128)(2,1)} %product.1), calls=%async_computation | async-start | bytes 1048576 | tf_op jit(solution)/shard_map/all_to_all | solution.py:98
  11.3 0.7 %copy-start.3 = (f32[3,32]{1,0:T(4,128)S(1)}, f32[3,32]{1,0:T(4,128)}, u32[]{:S(2)}) copy-start(f32[3,32]{1,0:T(4,128)} %param.11) | copy-start | bytes 1156
  26.6 9.8 %all-to-all-start.1 = ((f32[8,1,128]{2,1,0:T(1,128)}), f32[8,1,128]{2,1,0:T(1,128)S(1)}, u32[]{:S(2)}, u32[]{:S(2)}) async-start(f32[8,1,128]{2,1,0:T(1,128)} %bitcast.2), calls=%async_computation.1 | async-start | bytes 8192 | tf_op jit(solution)/shard_map/all_to_all | solution.py:115

commit v2 on v0

v2 whole, which is shorter than its diff:
```python
import functools
import math

import jax
import jax.numpy as jnp
import ml_dtypes
import numpy as np
from jax import lax
from jax.experimental import pallas as pl
from jax.experimental.pallas import tpu as pltpu
from jax.sharding import Mesh, PartitionSpec as P

NG = 30720
NTAU = 16
NATOM = 1000
GROUP = 16
LANES = 128
CORES = 2


def transform_matrix():
    steps = np.arange(NTAU, dtype=np.float64)
    table = np.cos(0.1 * 0.15 * 1.35 ** (steps[:, None] + steps[None, :])) / 4.0
    high = table.astype(ml_dtypes.bfloat16)
    low = (table - high.astype(np.float64)).astype(ml_dtypes.bfloat16)
    eye = np.eye(GROUP)
    return [np.kron(part.astype(np.float64), eye).astype(ml_dtypes.bfloat16) for part in (high, low)]


def product_kernel(chunks, occ_ref, virt_ref, out_ref, occ, virt, out, in_sems, out_sems):
    n_dest, _, _, width = out_ref.shape
    loads, stores = [], []
    for i, (t, rows) in enumerate(chunks):
        pair = [
            pltpu.make_async_copy(src.at[t, rows], dst.at[t, rows], in_sems.at[i, s])
            for s, (src, dst) in enumerate(((occ_ref, occ), (virt_ref, virt)))
        ]
        for load in pair:
            load.start()
        loads.append(pair)
    for i, (t, rows) in enumerate(chunks):
        for load in loads[i]:
            load.wait()
        product = occ[t, rows].astype(jnp.float32) * virt[t, rows].astype(jnp.float32)
        for j in range(n_dest):
            out[j, t, rows] = product[:, j * width : (j + 1) * width].astype(jnp.bfloat16)
        store = pltpu.make_async_copy(out.at[:, t, rows], out_ref.at[:, t, rows], out_sems.at[i])
        store.start()
        stores.append(store)
    for store in stores:
        store.wait()


def transform_kernel(high_ref, low_ref, in_ref, out_ref):
    n_out, rows, width = out_ref.shape
    for start in range(0, rows, GROUP):
        block = pl.ds(start, GROUP)
        terms = in_ref[:, block, :].reshape(NTAU * GROUP, width)
        total = jnp.dot(high_ref[...], terms, preferred_element_type=jnp.float32)
        total += jnp.dot(low_ref[...], terms, preferred_element_type=jnp.float32)
        out_ref[:, block, :] = total.reshape(n_out, GROUP, width).astype(out_ref.dtype)


def energy_kernel(prod_ref, adjoint_ref, weight_ref, label_ref, message_ref):
    n_time, rows, _ = prod_ref.shape
    terms = prod_ref[0].astype(jnp.float32) * adjoint_ref[0]
    for t in range(1, n_time):
        terms += prod_ref[t].astype(jnp.float32) * adjoint_ref[t]
    energy = jnp.sum(terms, axis=1, keepdims=True)
    row = lax.broadcasted_iota(jnp.int32, (rows, LANES), 0)
    lane = lax.broadcasted_iota(jnp.int32, (rows, LANES), 1)
    spread = jnp.sum(jnp.where(lane % rows == row, energy, 0.0), axis=0, keepdims=True)
    message = spread * weight_ref[...] + label_ref[...]
    message_ref[...] = jnp.broadcast_to(message, message_ref.shape)


def forces_kernel(rows, n_col, message_ref, forces_ref):
    sums = []
    for block in range(message_ref.shape[0] // n_col * CORES):
        pair, core = divmod(block, CORES)
        devices = pl.ds(pair * n_col, n_col)
        sums.append(jnp.sum(message_ref[devices, core, :], axis=0, keepdims=True))
    parts = [
        jnp.concatenate([total[:, p * rows : (p + 1) * rows] for total in sums], axis=1)
        for p in range(4)
    ]
    owners = parts[3].astype(jnp.int32)
    weights = jnp.concatenate(parts[:3] + [jnp.zeros_like(parts[0])] * 5, axis=0)
    upper, lower = owners // LANES, owners % LANES
    n_upper = pl.cdiv(NATOM, LANES)
    rest = jnp.concatenate([jnp.where(upper == u, weights, 0.0) for u in range(n_upper)], axis=0)
    lanes = lax.broadcasted_iota(jnp.int32, (LANES, owners.shape[1]), 0)
    onehot = jnp.where(lanes == lower, 1.0, 0.0).astype(jnp.bfloat16)
    forces = jnp.zeros((8 * n_upper, LANES), jnp.float32)
    for _ in range(3):
        part = rest.astype(jnp.bfloat16)
        rest = rest - part.astype(jnp.float32)
        forces += lax.dot_general(
            part, onehot, (((1,), (1,)), ((), ())), preferred_element_type=jnp.float32
        )
    for u in range(n_upper):
        count = min(LANES, NATOM - u * LANES)
        forces_ref[:, u * LANES : u * LANES + count] = forces[u * 8 : u * 8 + 3, :count]


def on_device(sizes, green_occ, green_virt, adjoint_w, grad_basis, owner_map, block_offset):
    n_pair, n_col, n_tm = sizes
    n_time, rows, columns = green_occ.shape
    width = columns // n_tm
    scale = 1.0 / math.sqrt(NTAU * NG)
    high, low = (jnp.asarray(part) for part in transform_matrix())
    shape = (NTAU, rows, width)

    half = rows // 2
    chunks = [(t, pl.ds(start, half)) for t in range(n_time) for start in (0, half)]
    product = pl.pallas_call(
        functools.partial(product_kernel, chunks),
        in_specs=[pl.BlockSpec(memory_space=pl.ANY)] * 2,
        out_specs=pl.BlockSpec(memory_space=pl.ANY),
        out_shape=jax.ShapeDtypeStruct((n_tm, n_time, rows, width), jnp.bfloat16),
        scratch_shapes=[
            pltpu.VMEM(green_occ.shape, jnp.bfloat16),
            pltpu.VMEM(green_virt.shape, jnp.bfloat16),
            pltpu.VMEM((n_tm, n_time, rows, width), jnp.bfloat16),
            pltpu.SemaphoreType.DMA((len(chunks), 2)),
            pltpu.SemaphoreType.DMA((len(chunks),)),
        ],
        name="product",
    )(green_occ, green_virt)
    times = lax.all_to_all(product, "tm", split_axis=0, concat_axis=0, tiled=True).reshape(shape)

    def transform(name, values, dtype):
        return pl.pallas_call(
            transform_kernel,
            out_shape=jax.ShapeDtypeStruct(shape, dtype),
            cost_estimate=pl.CostEstimate(
                flops=4 * NTAU * GROUP * rows * NTAU * width,
                bytes_accessed=(2 + jnp.dtype(dtype).itemsize) * NTAU * rows * width,
                transcendentals=0,
            ),
            compiler_params=pltpu.CompilerParams(vmem_limit_bytes=16 << 20),
            name=name,
        )(high, low, values)

    owners = lax.dynamic_slice_in_dim(owner_map, block_offset[0], rows, 0)
    weight = jnp.concatenate([grad_basis.reshape(3 * rows) * scale, jnp.zeros((rows,), jnp.float32)])
    label = jnp.concatenate(
        [jnp.zeros((3 * rows,), jnp.float32), owners.astype(jnp.float32) * (1.0 / (n_col * n_tm))]
    )
    adjoint_time = transform("adjoint_time", adjoint_w, jnp.float32)
    message = pl.pallas_call(
        energy_kernel,
        out_shape=jax.ShapeDtypeStruct((CORES * n_tm, LANES), jnp.float32),
        compiler_params=pltpu.CompilerParams(vmem_limit_bytes=16 << 20),
        name="energy",
    )(times, adjoint_time, weight[None, :], label[None, :])

    message = lax.all_to_all(message, ("core", "tm"), split_axis=0, concat_axis=0, tiled=True)
    chi_freq = transform("chi_freq", times, jnp.bfloat16)
    message = jnp.sum(message.reshape(CORES, n_tm, LANES), axis=1)
    message = jnp.broadcast_to(message[None], (n_pair * n_col, CORES, LANES))
    message = lax.all_to_all(message, ("pair", "col"), split_axis=0, concat_axis=0, tiled=True)
    forces = pl.pallas_call(
        functools.partial(forces_kernel, rows, n_col),
        out_shape=jax.ShapeDtypeStruct((3, NATOM), jnp.float32),
        compiler_params=pltpu.CompilerParams(vmem_limit_bytes=8 << 20),
        name="forces",
    )(message)
    return (chi_freq, forces)


def solution(mesh):
    n_row, n_col, n_tm = (mesh.shape[name] for name in ("row", "col", "tm"))
    n_pair = n_row // CORES
    fine = Mesh(mesh.devices.reshape(n_pair, CORES, n_col, n_tm), ("pair", "core", "col", "tm"))
    row = ("pair", "core")
    in_specs = (
        P("tm", row, "col"),
        P("tm", row, "col"),
        P(None, row, ("col", "tm")),
        P(None, row),
        P(),
        P(row),
    )
    out_specs = (P(None, row, ("col", "tm")), P())
    return jax.shard_map(
        functools.partial(on_device, (n_pair, n_col, n_tm)),
        mesh=fine,
        in_specs=in_specs,
        out_specs=out_specs,
        check_vma=False,
    )
```

time: 283 us -> 62.1 us (0.22)
  blocking collectives: 250 us -> 13.1 us
  starting transfers between devices: 7.65 us -> 20.7 us
  local copies, waits for them, and re-layouts: 8.71 us -> 0.81 us
  waiting for transfers between devices: 12.4 us -> 20.1 us
  Pallas kernels: 0 us -> 4.94 us
    psum x2 -> x0, blocking collectives: 250 us -> none  [the longest x1 196 us: on_device(): energy = lax.psum(partial_value, ('col', 'tm'))]
    all_to_all x0 -> x1, blocking collectives: none -> 13.1 us  [on_device(): lax.all_to_all(message, ('core', 'tm'), split_axis=0, concat_axis=0, tile...]
    all_to_all x1 -> x2, starting transfers between devices: 7.65 us -> 20.7 us  [the longest x1 12.9 us: on_device(): lax.all_to_all(message, ('pair', 'col'), split_axis=0, concat_axis=0, til...]
    all_to_all x1 -> x2, waiting for transfers between devices: 12.4 us -> 20.1 us  [the longest x1 12.7 us: on_device(): lax.all_to_all(product, 'tm', split_axis=0, concat_axis=0, tiled=True)]
    pallas_call x0 -> x5, Pallas kernels: none -> 4.94 us  [the longest x1 2.18 us: on_device(): pl.pallas_call(functools.partial(product_kernel, chunks), in_specs=[pl.Bl...]
    unnamed x7 -> x8, local copies, waits for them, and re-layouts: 4.61 us -> 0.03 us
  transfers between devices with their start and end apart: 1 -> 2, of which waited for: 1 -> 2; matrix products, arithmetic and copies ran while one was open for 0% -> 2% of each run, Pallas kernels for 0% -> 3%
where the time goes in v2:
time: 62.1 us; the launch traced here: 61.8 us
  starting transfers between devices  20.7 us (33%)
  waiting for transfers between devices  20.1 us (32%)
  blocking collectives  13.1 us (21%)
  Pallas kernels  4.94 us (8%)
  between operations  1.36 us (2%)
  local copies, waits for them, and re-layouts  0.81 us (1%)
  other arithmetic  0.8 us (1%)
    all_to_all x1, blocking collectives, on_device(): lax.all_to_all(message, ('core', 'tm'), split_axis=0, concat_axis=0, tile...  13.1 us
    all_to_all x1, starting transfers between devices, on_device(): lax.all_to_all(message, ('pair', 'col'), split_axis=0, concat_axis=0, til...  12.9 us
    all_to_all x1, waiting for transfers between devices, on_device(): lax.all_to_all(product, 'tm', split_axis=0, concat_axis=0, tiled=True)  12.7 us
    all_to_all x1, starting transfers between devices, on_device(): lax.all_to_all(product, 'tm', split_axis=0, concat_axis=0, tiled=True)  7.79 us
    all_to_all x1, waiting for transfers between devices, on_device(): lax.all_to_all(message, ('pair', 'col'), split_axis=0, concat_axis=0, til...  7.42 us
    pallas_call x1, Pallas kernels, on_device(): pl.pallas_call(functools.partial(product_kernel, chunks), in_specs=[pl.Bl...  2.18 us
    pallas_call x2, Pallas kernels, transform(): pl.pallas_call(transform_kernel, out_shape=jax.ShapeDtypeStruct(shape, dt...  1.67 us
  transfers between devices with their start and end apart: 2, of which 2 were waited for; matrix products, arithmetic and copies ran while one was open for 2% of the time, Pallas kernels for 3%

profile of v2, /device:TPU:1, one launch (start us, length us, event | category | flops | bytes accessed | tf_op | source)
XLA Modules:
  0.0 61.8 jit_solution(11934067258944486384)
XLA Ops:
  0.6 2.2 %product.1 = bf16[8,2,32,480]{3,2,1,0:T(8,128)(2,1)} custom-call(bf16[2,32,3840]{2,1,0:T(8,128)(2,1)} %occ_ref.1, bf16[2,32,3840]{2,1,0:T(8,128)(2,1)} %virt_ref.1), custom_call_target="tpu_custom_call" | custom-call | tf_op jit(solution)/shard_map/product/pallas_call | solution.py:116
  2.8 0.0 copy-start.3
  2.8 0.0 copy-start
  2.8 0.0 copy-start.1
  2.9 0.0 copy-start.2
  2.9 7.8 %all-to-all-start = ((bf16[8,2,32,480]{3,2,1,0:T(8,128)(2,1)}), bf16[8,2,32,480]{3,2,1,0:T(8,128)(2,1)S(1)}, u32[]{:S(2)}, u32[]{:S(2)}) async-start(bf16[8,2,32,480]{3,2,1,0:T(8,128)(2,1)} %product.1), calls=%async_computation | async-start | bytes 1048576 | tf_op jit(solution)/shard_map/all_to_all | solution.py:130
  11.3 0.0 copy-done.3
  11.3 0.1 mul.17
  11.4 0.0 copy-done
  11.4 0.0 copy-done.1
  11.4 0.0 copy-done.2
  11.4 0.4 adjoint_time.1.adjoint_ref
  11.9 0.8 %convert_multiply_fusion = f32[32]{0:T(128)S(1)} fusion(s32[30720]{0:T(1024)} %param.12, s32[]{:T(128)S(6)} %select_n.3), kind=kLoop, calls=%fused_computation.3 | loop fusion | flops 64 | bytes 260 | tf_op jit(solution)/shard_map/mul | solution.py:148
  12.6 0.1 pad_bitcast_fusion
  12.7 12.7 %all-to-all-done = bf16[8,2,32,480]{3,2,1,0:T(8,128)(2,1)S(1)} async-done(((bf16[8,2,32,480]{3,2,1,0:T(8,128)(2,1)}), bf16[8,2,32,480]{3,2,1,0:T(8,128)(2,1)S(1)}, u32[]{:S(2)}, u32[]{:S(2)}) %all-to-all-start) | async-done | bytes 491552 | tf_op jit(solution)/shard_map/all_to_all | solution.py:130
  25.4 0.2 energy.1
  25.6 13.1 %all_to_all.19 = f32[16,1,128]{2,1,0:T(1,128)S(1)} all-to-all(f32[16,1,128]{2,1,0:T(1,128)S(1)} %bitcast.17), channel_id=1, replica_groups=mesh['pair'=4,'core'=2,'col'=8,'tm'=8] {'core','tm'}, dimensions={0} | all-to-all | bytes 16384 | tf_op jit(solution)/shard_map/all_to_all | solution.py:158
  38.7 0.6 %broadcast_in_dim.16 = f32[32,2,128]{2,1,0:T(2,128)} broadcast(f32[2,128]{1,0:T(2,128)S(1)} %bitcast_reduce_fusion), dimensions={1,2} | broadcast | bytes 33792 | tf_op jit(solution)/shard_map/broadcast_in_dim | solution.py:161
  39.3 12.9 %all-to-all-start.2 = ((f32[32,2,128]{2,1,0:T(2,128)}), f32[32,2,128]{2,1,0:T(2,128)S(1)}, u32[]{:S(2)}, u32[]{:S(2)}) async-start(f32[32,2,128]{2,1,0:T(2,128)} %broadcast_in_dim.16), calls=%async_computation.2 | async-start | bytes 65536 | tf_op jit(solution)/shard_map/all_to_all | solution.py:162
  52.2 1.2 %chi_freq.1 = bf16[16,32,480]{2,1,0:T(8,128)(2,1)} custom-call(bf16[256,256]{1,0:T(8,128)(2,1)S(1)} %copy-done, bf16[256,256]{1,0:T(8,128)(2,1)S(1)} %copy-done.1, bf16[16,32,480]{2,1,0:T(8,128)(2,1)S(1)} %bitcast.16), custom_call_target="tpu_custom_call" | custom-call | flops 251658240 | bytes 983040 | tf_op jit(solution)/shard_map/chi_freq/pallas_call | solution.py:133
  53.4 7.4 %all-to-all-done.2.message_ref = f32[32,2,128]{2,1,0:T(2,128)S(1)} async-done(((f32[32,2,128]{2,1,0:T(2,128)}), f32[32,2,128]{2,1,0:T(2,128)S(1)}, u32[]{:S(2)}, u32[]{:S(2)}) %all-to-all-start.2) | async-done | bytes 32800 | tf_op jit(solution)/shard_map/all_to_all | solution.py:162
  60.9 0.9 %forces.1 = f32[3,1000]{1,0:T(4,128)} custom-call(f32[32,2,128]{2,1,0:T(2,128)S(1)} %all-to-all-done.2.message_ref), custom_call_target="tpu_custom_call" | custom-call | tf_op jit(solution)/shard_map/forces/pallas_call | solution.py:163
  (2 shorter events, 0.0 us)
Async XLA Ops:
  2.8 8.5 %copy-start.3 = (f32[3,32]{1,0:T(4,128)S(1)}, f32[3,32]{1,0:T(4,128)}, u32[]{:S(2)}) copy-start(f32[3,32]{1,0:T(4,128)} %param.11) | copy-start | bytes 1156
  2.8 8.6 %copy-start = (bf16[256,256]{1,0:T(8,128)(2,1)S(1)}, bf16[256,256]{1,0:T(8,128)(2,1)}, u32[]{:S(2)}) copy-start(bf16[256,256]{1,0:T(8,128)(2,1)} %constant.5.clone.high_ref) | copy-start | bytes 393220
  2.8 8.6 %copy-start.1 = (bf16[256,256]{1,0:T(8,128)(2,1)S(1)}, bf16[256,256]{1,0:T(8,128)(2,1)}, u32[]{:S(2)}) copy-start(bf16[256,256]{1,0:T(8,128)(2,1)} %constant.6.clone.low_ref) | copy-start | bytes 393220
  2.9 8.6 %copy-start.2 = (bf16[16,32,480]{2,1,0:T(8,128)(2,1)S(1)}, bf16[16,32,480]{2,1,0:T(8,128)(2,1)}, u32[]{:S(2)}) copy-start(bf16[16,32,480]{2,1,0:T(8,128)(2,1)} %in_ref.1) | copy-start | bytes 1474564
  2.9 22.5 %all-to-all-start = ((bf16[8,2,32,480]{3,2,1,0:T(8,128)(2,1)}), bf16[8,2,32,480]{3,2,1,0:T(8,128)(2,1)S(1)}, u32[]{:S(2)}, u32[]{:S(2)}) async-start(bf16[8,2,32,480]{3,2,1,0:T(8,128)(2,1)} %product.1), calls=%async_computation | async-start | bytes 1048576 | tf_op jit(solution)/shard_map/all_to_all | solution.py:130
  39.3 21.6 %all-to-all-start.2 = ((f32[32,2,128]{2,1,0:T(2,128)}), f32[32,2,128]{2,1,0:T(2,128)S(1)}, u32[]{:S(2)}, u32[]{:S(2)}) async-start(f32[32,2,128]{2,1,0:T(2,128)} %broadcast_in_dim.16), calls=%async_computation.2 | async-start | bytes 65536 | tf_op jit(solution)/shard_map/all_to_all | solution.py:162

commit v3 on v2

v3 whole, which is shorter than its diff:
```python
import functools
import math

import jax
import jax.numpy as jnp
import ml_dtypes
import numpy as np
from jax import lax
from jax.experimental import pallas as pl
from jax.experimental.pallas import tpu as pltpu
from jax.sharding import Mesh, PartitionSpec as P

NG = 30720
NTAU = 16
NATOM = 1000
GROUP = 16
LANES = 128
SHIFT = 32
QUARTERS = LANES // SHIFT
FULL = 3
CORES = 2


def transform_matrix():
    steps = np.arange(NTAU, dtype=np.float64)
    table = np.cos(0.1 * 0.15 * 1.35 ** (steps[:, None] + steps[None, :])) / 4.0
    high = table.astype(ml_dtypes.bfloat16)
    low = (table - high.astype(np.float64)).astype(ml_dtypes.bfloat16)
    eye = np.eye(GROUP)
    return [np.kron(part.astype(np.float64), eye).astype(ml_dtypes.bfloat16) for part in (high, low)]


def roll(values, shift):
    return pltpu.roll(values.astype(jnp.float32), shift, 1).astype(values.dtype)


def product_kernel(occ_ref, virt_ref, out_ref, occ, virt, out, in_sems, out_sems):
    n_dest = out_ref.shape[0]
    n_time, rows, _ = occ.shape
    blocks = [(t, pl.ds(start, GROUP)) for t in range(n_time) for start in range(0, rows, GROUP)]
    loads, stores = [], []
    for q, (t, block) in enumerate(blocks):
        pair = [
            pltpu.make_async_copy(src.at[t, block], dst.at[t, block], in_sems.at[q, s])
            for s, (src, dst) in enumerate(((occ_ref, occ), (virt_ref, virt)))
        ]
        for load in pair:
            load.start()
        loads.append(pair)

    def send(part, first, count):
        rows = pl.ds(first * GROUP, count * GROUP)
        store = pltpu.make_async_copy(out.at[:, rows], out_ref.at[:, rows], out_sems.at[part])
        store.start()
        stores.append(store)

    quarter = lax.broadcasted_iota(jnp.int32, (GROUP, LANES), 1) // SHIFT
    rests = {}
    for q, (t, block) in enumerate(blocks):
        for load in loads[q]:
            load.wait()

        def tile(k):
            columns = pl.ds(k * LANES, LANES)
            return occ[t, block, columns] * virt[t, block, columns]

        for j in range(n_dest):
            start = j * (FULL * QUARTERS + QUARTERS - 1)
            head = -start % QUARTERS
            hole = QUARTERS - 1 - head
            first = (start + head) // QUARTERS
            for m in range(FULL):
                out[j, pl.ds((q * FULL + m) * GROUP, GROUP), :] = tile(first + m)
            if head == 0:
                rest = tile(first + FULL)
            elif hole == 0:
                rest = tile(first - 1)
            else:
                rest = jnp.where(quarter > hole, tile(first - 1), tile(first + FULL))
            rests[j, q] = rest
        if q < len(blocks) - 1:
            send(q, q * FULL, FULL)
            continue
        for j in range(n_dest):
            hole = QUARTERS - 1 - -j * (FULL * QUARTERS + QUARTERS - 1) % QUARTERS
            for m in range(FULL):
                moved = roll(rests[j, q], LANES - (1 + m) * SHIFT)
                filled = jnp.where(quarter == hole, moved, rests[j, m])
                out[j, pl.ds(((q + 1) * FULL + m) * GROUP, GROUP), :] = filled
        send(q, q * FULL, 2 * FULL)
    for store in stores:
        store.wait()


def own_place():
    head = lax.rem(lax.axis_index("tm"), QUARTERS)
    return head, QUARTERS - 1 - head


def transformed(high_ref, low_ref, values):
    total = jnp.dot(high_ref[...], values, preferred_element_type=jnp.float32)
    return total + jnp.dot(low_ref[...], values, preferred_element_type=jnp.float32)


def adjoint_kernel(high_ref, low_ref, adjoint_ref, out_ref):
    n_freq, rows, width = adjoint_ref.shape
    n_source = out_ref.shape[0]
    per_source, halves = n_freq // n_source, rows // GROUP
    n_block = per_source * halves
    head, hole = own_place()
    split = LANES - head * SHIFT
    quarter = lax.broadcasted_iota(jnp.int32, (GROUP, LANES), 1) // SHIFT
    wide = lax.broadcasted_iota(jnp.int32, (n_freq * GROUP, LANES), 1)
    rests = {}
    for half in range(halves):
        block = pl.ds(half * GROUP, GROUP)
        values = adjoint_ref[:, block, :].reshape(n_freq * GROUP, width)
        total = transformed(high_ref, low_ref, values)
        pad = jnp.zeros((n_freq * GROUP, (FULL + 1) * LANES - width), jnp.float32)
        total = jnp.concatenate([total, pad], axis=1)
        turned = [
            pltpu.roll(total[:, m * LANES : (m + 1) * LANES], lax.rem(split, LANES), 1)
            for m in range(FULL + 1)
        ]
        packed = [jnp.where(wide < split, turned[m], turned[m + 1]) for m in range(FULL)]
        rest = jnp.where(wide < split, turned[FULL], turned[0])
        for t in range(n_freq):
            i, tt = divmod(t, per_source)
            q = tt * halves + half
            lines = slice(t * GROUP, (t + 1) * GROUP)
            for m in range(FULL):
                out_ref[i, pl.ds((q * FULL + m) * GROUP, GROUP), :] = packed[m][lines]
            rests[i, q] = rest[lines]
    for i in range(n_source):
        for m in range(FULL):
            moved = pltpu.roll(rests[i, n_block - 1], LANES - (1 + m) * SHIFT, 1)
            filled = jnp.where(quarter == hole, moved, rests[i, m])
            out_ref[i, pl.ds((n_block * FULL + m) * GROUP, GROUP), :] = filled


def energy_kernel(rows, times_ref, adjoint_ref, weight_ref, label_ref, message_ref):
    n_source, lines, _ = times_ref.shape
    n_block = lines // GROUP // FULL - 1
    halves = rows // GROUP
    _, hole = own_place()
    in_hole = lax.broadcasted_iota(jnp.int32, (GROUP, LANES), 1) // SHIFT == hole
    sums = [jnp.zeros((GROUP, LANES), jnp.float32) for _ in range(halves)]

    def terms(tile):
        lines = pl.ds(tile * GROUP, GROUP)
        total = jnp.zeros((GROUP, LANES), jnp.float32)
        for i in range(n_source):
            total += times_ref[i, lines, :].astype(jnp.float32) * adjoint_ref[i, lines, :]
        return total

    for q in range(n_block):
        for m in range(FULL):
            sums[q % halves] += terms(q * FULL + m)
    for m in range(FULL):
        rest = terms(n_block * FULL + m)
        sums[m % halves] += jnp.where(in_hole, 0.0, rest)
        sums[(n_block - 1) % halves] += jnp.where(in_hole, rest, 0.0)
    total = jnp.zeros((1, LANES), jnp.float32)
    for half in range(halves):
        energy = jnp.sum(sums[half], axis=1, keepdims=True)
        row = lax.broadcasted_iota(jnp.int32, (GROUP, LANES), 0) + half * GROUP
        lane = lax.broadcasted_iota(jnp.int32, (GROUP, LANES), 1)
        total += jnp.sum(jnp.where(lane % rows == row, energy, 0.0), axis=0, keepdims=True)
    message = total * weight_ref[...] + label_ref[...]
    message_ref[...] = jnp.broadcast_to(message, message_ref.shape)


def chi_kernel(high_ref, low_ref, times_ref, chi_ref):
    n_source = times_ref.shape[0]
    n_freq, rows, width = chi_ref.shape
    head, hole = own_place()
    turn = head * SHIFT
    quarter = lax.broadcasted_iota(jnp.int32, (GROUP, LANES), 1) // SHIFT
    wide = lax.broadcasted_iota(jnp.int32, (n_freq * GROUP, LANES), 1)
    n_block = NTAU // n_source * (rows // GROUP)

    def stored(i, tile):
        return times_ref[i, pl.ds(tile * GROUP, GROUP), :]

    def last_rest(i):
        rest = stored(i, n_block * FULL)
        for m in range(FULL):
            moved = roll(stored(i, n_block * FULL + m), (1 + m) * SHIFT)
            rest = jnp.where(quarter == lax.rem(hole + 1 + m, QUARTERS), moved, rest)
        return rest

    def column_tile(half, m):
        parts = []
        for t in range(NTAU):
            i, tt = divmod(t, NTAU // n_source)
            q = tt * (rows // GROUP) + half
            if m < FULL:
                parts.append(stored(i, q * FULL + m))
            elif q < n_block - 1:
                parts.append(stored(i, n_block * FULL + q))
            else:
                parts.append(last_rest(i))
        return jnp.concatenate(parts, axis=0)

    for half in range(rows // GROUP):
        block = pl.ds(half * GROUP, GROUP)
        values = jnp.concatenate([column_tile(half, m) for m in range(FULL + 1)], axis=1)
        chi = transformed(high_ref, low_ref, values)
        turned = [pltpu.roll(chi[:, m * LANES : (m + 1) * LANES], turn, 1) for m in range(FULL + 1)]
        for m in range(FULL + 1):
            count = min(LANES, width - m * LANES)
            natural = jnp.where(wide < turn, turned[m - 1], turned[m])[:, :count]
            natural = natural.astype(jnp.bfloat16).reshape(n_freq, GROUP, count)
            chi_ref[:, block, pl.ds(m * LANES, count)] = natural


def forces_kernel(rows, n_col, message_ref, forces_ref):
    sums = []
    for block in range(message_ref.shape[0] // n_col * CORES):
        pair, core = divmod(block, CORES)
        devices = pl.ds(pair * n_col, n_col)
        sums.append(jnp.sum(message_ref[devices, core, :], axis=0, keepdims=True))
    parts = [
        jnp.concatenate([total[:, p * rows : (p + 1) * rows] for total in sums], axis=1)
        for p in range(4)
    ]
    owners = parts[3].astype(jnp.int32)
    weights = jnp.concatenate(parts[:3] + [jnp.zeros_like(parts[0])] * 5, axis=0)
    upper, lower = owners // LANES, owners % LANES
    n_upper = pl.cdiv(NATOM, LANES)
    rest = jnp.concatenate([jnp.where(upper == u, weights, 0.0) for u in range(n_upper)], axis=0)
    lanes = lax.broadcasted_iota(jnp.int32, (LANES, owners.shape[1]), 0)
    onehot = jnp.where(lanes == lower, 1.0, 0.0).astype(jnp.bfloat16)
    forces = jnp.zeros((8 * n_upper, LANES), jnp.float32)
    for _ in range(3):
        part = rest.astype(jnp.bfloat16)
        rest = rest - part.astype(jnp.float32)
        forces += lax.dot_general(
            part, onehot, (((1,), (1,)), ((), ())), preferred_element_type=jnp.float32
        )
    for u in range(n_upper):
        count = min(LANES, NATOM - u * LANES)
        forces_ref[:, u * LANES : u * LANES + count] = forces[u * 8 : u * 8 + 3, :count]


def on_device(sizes, green_occ, green_virt, adjoint_w, grad_basis, owner_map, block_offset):
    n_pair, n_col, n_tm = sizes
    n_time, rows, columns = green_occ.shape
    width = columns // n_tm
    high, low = (jnp.asarray(part) for part in transform_matrix())
    n_block = n_time * rows // GROUP
    tiles = n_block * FULL + FULL
    assert width == FULL * LANES + (QUARTERS - 1) * SHIFT and n_block == FULL + 1

    packed = (n_tm, tiles * GROUP, LANES)
    product = pl.pallas_call(
        product_kernel,
        in_specs=[pl.BlockSpec(memory_space=pl.ANY)] * 2,
        out_specs=pl.BlockSpec(memory_space=pl.ANY),
        out_shape=jax.ShapeDtypeStruct(packed, jnp.bfloat16),
        scratch_shapes=[
            pltpu.VMEM(green_occ.shape, jnp.bfloat16),
            pltpu.VMEM(green_virt.shape, jnp.bfloat16),
            pltpu.VMEM(packed, jnp.bfloat16),
            pltpu.SemaphoreType.DMA((n_block, 2)),
            pltpu.SemaphoreType.DMA((n_block,)),
        ],
        compiler_params=pltpu.CompilerParams(vmem_limit_bytes=60 << 20),
        name="product",
    )(green_occ, green_virt)
    times = lax.all_to_all(product, "tm", split_axis=0, concat_axis=0, tiled=True)

    def kernel(body, name, shape, dtype, limit, *operands):
        elements = NTAU * rows * width
        return pl.pallas_call(
            body,
            out_shape=jax.ShapeDtypeStruct(shape, dtype),
            cost_estimate=pl.CostEstimate(
                flops=4 * NTAU * GROUP * elements, bytes_accessed=4 * elements, transcendentals=0
            ),
            compiler_params=pltpu.CompilerParams(vmem_limit_bytes=limit << 20),
            name=name,
        )(*operands)

    scale = 1.0 / math.sqrt(NTAU * NG)
    owners = lax.dynamic_slice_in_dim(owner_map, block_offset[0], rows, 0)
    weight = jnp.concatenate([grad_basis.reshape(3 * rows) * scale, jnp.zeros((rows,), jnp.float32)])
    label = jnp.concatenate(
        [jnp.zeros((3 * rows,), jnp.float32), owners.astype(jnp.float32) * (1.0 / (n_col * n_tm))]
    )
    adjoint = kernel(adjoint_kernel, "adjoint", packed, jnp.float32, 16, high, low, adjoint_w)
    message = pl.pallas_call(
        functools.partial(energy_kernel, rows),
        out_shape=jax.ShapeDtypeStruct((CORES * n_tm, LANES), jnp.float32),
        compiler_params=pltpu.CompilerParams(vmem_limit_bytes=16 << 20),
        name="energy",
    )(times, adjoint, weight[None, :], label[None, :])

    message = lax.all_to_all(message, ("core", "tm"), split_axis=0, concat_axis=0, tiled=True)
    chi_freq = kernel(
        chi_kernel, "chi_freq", (NTAU, rows, width), jnp.bfloat16, 16, high, low, times
    )
    message = jnp.sum(message.reshape(CORES, n_tm, LANES), axis=1)
    message = jnp.broadcast_to(message[None], (n_pair * n_col, CORES, LANES))
    message = lax.all_to_all(message, ("pair", "col"), split_axis=0, concat_axis=0, tiled=True)
    forces = pl.pallas_call(
        functools.partial(forces_kernel, rows, n_col),
        out_shape=jax.ShapeDtypeStruct((3, NATOM), jnp.float32),
        compiler_params=pltpu.CompilerParams(vmem_limit_bytes=8 << 20),
        name="forces",
    )(message)
    return (chi_freq, forces)


def solution(mesh):
    n_row, n_col, n_tm = (mesh.shape[name] for name in ("row", "col", "tm"))
    n_pair = n_row // CORES
    fine = Mesh(mesh.devices.reshape(n_pair, CORES, n_col, n_tm), ("pair", "core", "col", "tm"))
    row = ("pair", "core")
    in_specs = (
        P("tm", row, "col"),
        P("tm", row, "col"),
        P(None, row, ("col", "tm")),
        P(None, row),
        P(),
        P(row),
    )
    out_specs = (P(None, row, ("col", "tm")), P())
    return jax.shard_map(
        functools.partial(on_device, (n_pair, n_col, n_tm)),
        mesh=fine,
        in_specs=in_specs,
        out_specs=out_specs,
        check_vma=False,
    )
```

time: 62.1 us -> 61.4 us (0.989)
  waiting for transfers between devices: 20.1 us -> 19 us
    all_to_all x1, waiting for transfers between devices: 12.7 us -> 11.6 us  [on_device(): lax.all_to_all(product, 'tm', split_axis=0, concat_axis=0, tiled=True)]
where the time goes in v3:
time: 61.4 us; the launch traced here: 61 us
  starting transfers between devices  20.7 us (34%)
  waiting for transfers between devices  19 us (31%)
  blocking collectives  13.2 us (21%)
  Pallas kernels  5.22 us (9%)
  between operations  1.35 us (2%)
  local copies, waits for them, and re-layouts  0.81 us (1%)
  other arithmetic  0.8 us (1%)
    all_to_all x1, blocking collectives, on_device(): lax.all_to_all(message, ('core', 'tm'), split_axis=0, concat_axis=0, tile...  13.2 us
    all_to_all x1, starting transfers between devices, on_device(): lax.all_to_all(message, ('pair', 'col'), split_axis=0, concat_axis=0, til...  12.9 us
    all_to_all x1, waiting for transfers between devices, on_device(): lax.all_to_all(product, 'tm', split_axis=0, concat_axis=0, tiled=True)  11.6 us
    all_to_all x1, starting transfers between devices, on_device(): lax.all_to_all(product, 'tm', split_axis=0, concat_axis=0, tiled=True)  7.79 us
    all_to_all x1, waiting for transfers between devices, on_device(): lax.all_to_all(message, ('pair', 'col'), split_axis=0, concat_axis=0, til...  7.34 us
    pallas_call x1, Pallas kernels, on_device(): pl.pallas_call(product_kernel, in_specs=[pl.BlockSpec(memory_space=pl.ANY...  2.16 us
    pallas_call x2, Pallas kernels, kernel(): pl.pallas_call(body, out_shape=jax.ShapeDtypeStruct(shape, dtype), cost_e...  1.96 us
  transfers between devices with their start and end apart: 2, of which 2 were waited for; matrix products, arithmetic and copies ran while one was open for 2% of the time, Pallas kernels for 3%

profile of v3, /device:TPU:1, one launch (start us, length us, event | category | flops | bytes accessed | tf_op | source)
XLA Modules:
  0.0 61.0 jit_solution(7700425178400788236)
XLA Ops:
  0.6 2.2 %product.1 = bf16[8,240,128]{2,1,0:T(8,128)(2,1)} custom-call(bf16[2,32,3840]{2,1,0:T(8,128)(2,1)} %occ_ref.1, bf16[2,32,3840]{2,1,0:T(8,128)(2,1)} %virt_ref.1), custom_call_target="tpu_custom_call" | custom-call | tf_op jit(solution)/shard_map/product/pallas_call | solution.py:256
  2.8 0.0 copy-start.3
  2.8 0.0 copy-start
  2.8 0.0 copy-start.1
  2.8 0.0 copy-start.2
  2.8 7.8 %all-to-all-start = ((bf16[8,240,128]{2,1,0:T(8,128)(2,1)}), bf16[8,240,128]{2,1,0:T(8,128)(2,1)S(1)}, u32[]{:S(2)}, u32[]{:S(2)}) async-start(bf16[8,240,128]{2,1,0:T(8,128)(2,1)} %product.1), calls=%async_computation | async-start | bytes 983040 | tf_op jit(solution)/shard_map/all_to_all | solution.py:271
  11.3 0.0 copy-done.3
  11.3 0.1 mul.17
  11.4 0.0 copy-done
  11.4 0.0 copy-done.1
  11.4 0.0 copy-done.2
  11.4 0.6 %adjoint.1.adjoint_ref = f32[8,240,128]{2,1,0:T(8,128)S(1)} custom-call(bf16[256,256]{1,0:T(8,128)(2,1)S(1)} %copy-done.1, bf16[256,256]{1,0:T(8,128)(2,1)S(1)} %copy-done.2, bf16[16,32,480]{2,1,0:T(8,128)(2,1)S(1)} %copy-done), custom_call_target="tpu_custom_call" | custom-call | flops 251658240 | bytes 983040 | tf_op jit(solution)/shard_map/adjoint/pallas_call | solution.py:275
  12.0 0.8 %convert_multiply_fusion = f32[32]{0:T(128)S(1)} fusion(s32[30720]{0:T(1024)} %param.12, s32[]{:T(128)S(6)} %select_n.3), kind=kLoop, calls=%fused_computation.3 | loop fusion | flops 64 | bytes 260 | tf_op jit(solution)/shard_map/mul | solution.py:289
  12.8 0.1 pad_bitcast_fusion
  12.9 11.6 %all-to-all-done.times_ref = bf16[8,240,128]{2,1,0:T(8,128)(2,1)S(1)} async-done(((bf16[8,240,128]{2,1,0:T(8,128)(2,1)}), bf16[8,240,128]{2,1,0:T(8,128)(2,1)S(1)}, u32[]{:S(2)}, u32[]{:S(2)}) %all-to-all-start) | async-done | bytes 491552 | tf_op jit(solution)/shard_map/all_to_all | solution.py:271
  24.5 0.2 energy.1
  24.7 13.2 %all_to_all.19 = f32[16,1,128]{2,1,0:T(1,128)S(1)} all-to-all(f32[16,1,128]{2,1,0:T(1,128)S(1)} %bitcast.14), channel_id=1, replica_groups=mesh['pair'=4,'core'=2,'col'=8,'tm'=8] {'core','tm'}, dimensions={0} | all-to-all | bytes 16384 | tf_op jit(solution)/shard_map/all_to_all | solution.py:299
  38.0 0.6 %broadcast_in_dim.16 = f32[32,2,128]{2,1,0:T(2,128)} broadcast(f32[2,128]{1,0:T(2,128)S(1)} %bitcast_reduce_fusion), dimensions={1,2} | broadcast | bytes 33792 | tf_op jit(solution)/shard_map/broadcast_in_dim | solution.py:304
  38.6 12.9 %all-to-all-start.2 = ((f32[32,2,128]{2,1,0:T(2,128)}), f32[32,2,128]{2,1,0:T(2,128)S(1)}, u32[]{:S(2)}, u32[]{:S(2)}) async-start(f32[32,2,128]{2,1,0:T(2,128)} %broadcast_in_dim.16), calls=%async_computation.2 | async-start | bytes 65536 | tf_op jit(solution)/shard_map/all_to_all | solution.py:305
  51.5 1.3 %chi_freq.1 = bf16[16,32,480]{2,1,0:T(8,128)(2,1)} custom-call(bf16[256,256]{1,0:T(8,128)(2,1)S(1)} %copy-done.1, bf16[256,256]{1,0:T(8,128)(2,1)S(1)} %copy-done.2, bf16[8,240,128]{2,1,0:T(8,128)(2,1)S(1)} %all-to-all-done.times_ref), custom_call_target="tpu_custom_call" | custom-call | flops 251658240 | bytes 983040 | tf_op jit(solution)/shard_map/chi_freq/pallas_call | solution.py:275
  52.8 7.3 %all-to-all-done.2.message_ref = f32[32,2,128]{2,1,0:T(2,128)S(1)} async-done(((f32[32,2,128]{2,1,0:T(2,128)}), f32[32,2,128]{2,1,0:T(2,128)S(1)}, u32[]{:S(2)}, u32[]{:S(2)}) %all-to-all-start.2) | async-done | bytes 32800 | tf_op jit(solution)/shard_map/all_to_all | solution.py:305
  60.1 0.9 %forces.1 = f32[3,1000]{1,0:T(4,128)} custom-call(f32[32,2,128]{2,1,0:T(2,128)S(1)} %all-to-all-done.2.message_ref), custom_call_target="tpu_custom_call" | custom-call | tf_op jit(solution)/shard_map/forces/pallas_call | solution.py:306
  (2 shorter events, 0.0 us)
Async XLA Ops:
  2.8 8.5 %copy-start.3 = (f32[3,32]{1,0:T(4,128)S(1)}, f32[3,32]{1,0:T(4,128)}, u32[]{:S(2)}) copy-start(f32[3,32]{1,0:T(4,128)} %param.11) | copy-start | bytes 1156
  2.8 8.6 %copy-start = (bf16[16,32,480]{2,1,0:T(8,128)(2,1)S(1)}, bf16[16,32,480]{2,1,0:T(8,128)(2,1)}, u32[]{:S(2)}) copy-start(bf16[16,32,480]{2,1,0:T(8,128)(2,1)} %adjoint_ref.1) | copy-start | bytes 1474564
  2.8 8.6 %copy-start.1 = (bf16[256,256]{1,0:T(8,128)(2,1)S(1)}, bf16[256,256]{1,0:T(8,128)(2,1)}, u32[]{:S(2)}) copy-start(bf16[256,256]{1,0:T(8,128)(2,1)} %constant.5.clone.high_ref) | copy-start | bytes 393220
  2.8 8.6 %copy-start.2 = (bf16[256,256]{1,0:T(8,128)(2,1)S(1)}, bf16[256,256]{1,0:T(8,128)(2,1)}, u32[]{:S(2)}) copy-start(bf16[256,256]{1,0:T(8,128)(2,1)} %constant.6.clone.low_ref) | copy-start | bytes 393220
  2.8 21.7 %all-to-all-start = ((bf16[8,240,128]{2,1,0:T(8,128)(2,1)}), bf16[8,240,128]{2,1,0:T(8,128)(2,1)S(1)}, u32[]{:S(2)}, u32[]{:S(2)}) async-start(bf16[8,240,128]{2,1,0:T(8,128)(2,1)} %product.1), calls=%async_computation | async-start | bytes 983040 | tf_op jit(solution)/shard_map/all_to_all | solution.py:271
  38.6 21.6 %all-to-all-start.2 = ((f32[32,2,128]{2,1,0:T(2,128)}), f32[32,2,128]{2,1,0:T(2,128)S(1)}, u32[]{:S(2)}, u32[]{:S(2)}) async-start(f32[32,2,128]{2,1,0:T(2,128)} %broadcast_in_dim.16), calls=%async_computation.2 | async-start | bytes 65536 | tf_op jit(solution)/shard_map/all_to_all | solution.py:305

commit v4 on v3

--- a/solution.py
+++ b/solution.py
@@ -19,6 +19,7 @@
 QUARTERS = LANES // SHIFT
 FULL = 3
 CORES = 2
+FAR = 2
 
 
 def transform_matrix():
@@ -244,7 +245,8 @@
 
 
 def on_device(sizes, green_occ, green_virt, adjoint_w, grad_basis, owner_map, block_offset):
-    n_pair, n_col, n_tm = sizes
+    n_pair, n_near, n_tm = sizes
+    n_col = n_near * FAR
     n_time, rows, columns = green_occ.shape
     width = columns // n_tm
     high, low = (jnp.asarray(part) for part in transform_matrix())
@@ -291,20 +293,20 @@
     adjoint = kernel(adjoint_kernel, "adjoint", packed, jnp.float32, 16, high, low, adjoint_w)
     message = pl.pallas_call(
         functools.partial(energy_kernel, rows),
-        out_shape=jax.ShapeDtypeStruct((CORES * n_tm, LANES), jnp.float32),
+        out_shape=jax.ShapeDtypeStruct((CORES * n_near * n_tm, LANES), jnp.float32),
         compiler_params=pltpu.CompilerParams(vmem_limit_bytes=16 << 20),
         name="energy",
     )(times, adjoint, weight[None, :], label[None, :])
 
-    message = lax.all_to_all(message, ("core", "tm"), split_axis=0, concat_axis=0, tiled=True)
+    message = lax.all_to_all(message, ("core", "near", "tm"), split_axis=0, concat_axis=0, tiled=True)
     chi_freq = kernel(
         chi_kernel, "chi_freq", (NTAU, rows, width), jnp.bfloat16, 16, high, low, times
     )
-    message = jnp.sum(message.reshape(CORES, n_tm, LANES), axis=1)
-    message = jnp.broadcast_to(message[None], (n_pair * n_col, CORES, LANES))
-    message = lax.all_to_all(message, ("pair", "col"), split_axis=0, concat_axis=0, tiled=True)
+    message = jnp.sum(message.reshape(CORES, n_near * n_tm, LANES), axis=1)
+    message = jnp.broadcast_to(message[None], (n_pair * FAR, CORES, LANES))
+    message = lax.all_to_all(message, ("pair", "far"), split_axis=0, concat_axis=0, tiled=True)
     forces = pl.pallas_call(
-        functools.partial(forces_kernel, rows, n_col),
+        functools.partial(forces_kernel, rows, FAR),
         out_shape=jax.ShapeDtypeStruct((3, NATOM), jnp.float32),
         compiler_params=pltpu.CompilerParams(vmem_limit_bytes=8 << 20),
         name="forces",
@@ -315,19 +317,21 @@
 def solution(mesh):
     n_row, n_col, n_tm = (mesh.shape[name] for name in ("row", "col", "tm"))
     n_pair = n_row // CORES
-    fine = Mesh(mesh.devices.reshape(n_pair, CORES, n_col, n_tm), ("pair", "core", "col", "tm"))
-    row = ("pair", "core")
+    n_near = n_col // FAR
+    axes = ("pair", "core", "near", "far", "tm")
+    fine = Mesh(mesh.devices.reshape(n_pair, CORES, n_near, FAR, n_tm), axes)
+    row, col = ("pair", "core"), ("near", "far")
     in_specs = (
-        P("tm", row, "col"),
-        P("tm", row, "col"),
-        P(None, row, ("col", "tm")),
+        P("tm", row, col),
+        P("tm", row, col),
+        P(None, row, col + ("tm",)),
         P(None, row),
         P(),
         P(row),
     )
-    out_specs = (P(None, row, ("col", "tm")), P())
+    out_specs = (P(None, row, col + ("tm",)), P())
     return jax.shard_map(
-        functools.partial(on_device, (n_pair, n_col, n_tm)),
+        functools.partial(on_device, (n_pair, n_near, n_tm)),
         mesh=fine,
         in_specs=in_specs,
         out_specs=out_specs,

time: 61.4 us -> 60.8 us (level)
  blocking collectives: 13.2 us -> 17.7 us
  starting transfers between devices: 20.7 us -> 17.8 us
  waiting for transfers between devices: 19 us -> 16.8 us
    all_to_all x1, blocking collectives: 13.2 us -> 17.7 us  [on_device(): lax.all_to_all(message, ('core', 'near', 'tm'), split_axis=0, concat_axis...]
    all_to_all x1, starting transfers between devices: 12.9 us -> 10 us  [on_device(): lax.all_to_all(message, ('pair', 'far'), split_axis=0, concat_axis=0, til...]
    all_to_all x1, waiting for transfers between devices: 7.34 us -> 5.21 us  [on_device(): lax.all_to_all(message, ('pair', 'far'), split_axis=0, concat_axis=0, til...]
where the time goes in v4:
time: 60.8 us; the launch traced here: 60.5 us
  starting transfers between devices  17.8 us (29%)
  blocking collectives  17.7 us (29%)
  waiting for transfers between devices  16.8 us (28%)
  Pallas kernels  5.21 us (9%)
  between operations  1.34 us (2%)
  other arithmetic  0.8 us (1%)
  local copies, waits for them, and re-layouts  0.79 us (1%)
    all_to_all x1, blocking collectives, on_device(): lax.all_to_all(message, ('core', 'near', 'tm'), split_axis=0, concat_axis...  17.7 us
    all_to_all x1, waiting for transfers between devices, on_device(): lax.all_to_all(product, 'tm', split_axis=0, concat_axis=0, tiled=True)  11.6 us
    all_to_all x1, starting transfers between devices, on_device(): lax.all_to_all(message, ('pair', 'far'), split_axis=0, concat_axis=0, til...  10 us
    all_to_all x1, starting transfers between devices, on_device(): lax.all_to_all(product, 'tm', split_axis=0, concat_axis=0, tiled=True)  7.79 us
    all_to_all x1, waiting for transfers between devices, on_device(): lax.all_to_all(message, ('pair', 'far'), split_axis=0, concat_axis=0, til...  5.21 us
    pallas_call x1, Pallas kernels, on_device(): pl.pallas_call(product_kernel, in_specs=[pl.BlockSpec(memory_space=pl.ANY...  2.16 us
    pallas_call x2, Pallas kernels, kernel(): pl.pallas_call(body, out_shape=jax.ShapeDtypeStruct(shape, dtype), cost_e...  1.96 us
  transfers between devices with their start and end apart: 2, of which 2 were waited for; matrix products, arithmetic and copies ran while one was open for 2% of the time, Pallas kernels for 3%

profile of v4, /device:TPU:1, one launch (start us, length us, event | category | flops | bytes accessed | tf_op | source)
XLA Modules:
  0.0 60.5 jit_solution(17682200085037682438)
XLA Ops:
  0.6 2.2 %product.1 = bf16[8,240,128]{2,1,0:T(8,128)(2,1)} custom-call(bf16[2,32,3840]{2,1,0:T(8,128)(2,1)} %occ_ref.1, bf16[2,32,3840]{2,1,0:T(8,128)(2,1)} %virt_ref.1), custom_call_target="tpu_custom_call" | custom-call | tf_op jit(solution)/shard_map/product/pallas_call | solution.py:258
  2.8 0.0 copy-start.3
  2.8 0.0 copy-start
  2.8 0.0 copy-start.1
  2.8 0.0 copy-start.2
  2.8 7.8 %all-to-all-start = ((bf16[8,240,128]{2,1,0:T(8,128)(2,1)}), bf16[8,240,128]{2,1,0:T(8,128)(2,1)S(1)}, u32[]{:S(2)}, u32[]{:S(2)}) async-start(bf16[8,240,128]{2,1,0:T(8,128)(2,1)} %product.1), calls=%async_computation | async-start | bytes 983040 | tf_op jit(solution)/shard_map/all_to_all | solution.py:273
  11.3 0.0 copy-done.3
  11.3 0.1 mul.17
  11.4 0.0 copy-done
  11.4 0.0 copy-done.1
  11.4 0.0 copy-done.2
  11.4 0.6 %adjoint.1.adjoint_ref = f32[8,240,128]{2,1,0:T(8,128)S(1)} custom-call(bf16[256,256]{1,0:T(8,128)(2,1)S(1)} %copy-done.1, bf16[256,256]{1,0:T(8,128)(2,1)S(1)} %copy-done.2, bf16[16,32,480]{2,1,0:T(8,128)(2,1)S(1)} %copy-done), custom_call_target="tpu_custom_call" | custom-call | flops 251658240 | bytes 983040 | tf_op jit(solution)/shard_map/adjoint/pallas_call | solution.py:277
  12.0 0.8 %convert_multiply_fusion = f32[32]{0:T(128)S(1)} fusion(s32[30720]{0:T(1024)} %param.12, s32[]{:T(128)S(6)} %select_n.3), kind=kLoop, calls=%fused_computation.3 | loop fusion | flops 64 | bytes 260 | tf_op jit(solution)/shard_map/mul | solution.py:291
  12.8 0.1 pad_bitcast_fusion
  12.9 11.6 %all-to-all-done.times_ref = bf16[8,240,128]{2,1,0:T(8,128)(2,1)S(1)} async-done(((bf16[8,240,128]{2,1,0:T(8,128)(2,1)}), bf16[8,240,128]{2,1,0:T(8,128)(2,1)S(1)}, u32[]{:S(2)}, u32[]{:S(2)}) %all-to-all-start) | async-done | bytes 491552 | tf_op jit(solution)/shard_map/all_to_all | solution.py:273
  24.5 0.2 energy.1
  24.7 17.7 %all_to_all.19 = f32[64,1,128]{2,1,0:T(1,128)S(1)} all-to-all(f32[64,1,128]{2,1,0:T(1,128)S(1)} %bitcast.14), channel_id=1, replica_groups=mesh['pair'=4,'core'=2,'near'=4,'far'=2,'tm'=8] {'core','near','tm'}, dimensions={0} | all-to-all | bytes 65536 | tf_op jit(solution)/shard_map/all_to_all | solution.py:301
  42.4 0.6 broadcast_in_dim.16
  43.0 10.0 %all-to-all-start.2 = ((f32[8,2,128]{2,1,0:T(2,128)}), f32[8,2,128]{2,1,0:T(2,128)S(1)}, u32[]{:S(2)}, u32[]{:S(2)}) async-start(f32[8,2,128]{2,1,0:T(2,128)} %broadcast_in_dim.16), calls=%async_computation.2 | async-start | bytes 16384 | tf_op jit(solution)/shard_map/all_to_all | solution.py:307
  53.0 1.3 %chi_freq.1 = bf16[16,32,480]{2,1,0:T(8,128)(2,1)} custom-call(bf16[256,256]{1,0:T(8,128)(2,1)S(1)} %copy-done.1, bf16[256,256]{1,0:T(8,128)(2,1)S(1)} %copy-done.2, bf16[8,240,128]{2,1,0:T(8,128)(2,1)S(1)} %all-to-all-done.times_ref), custom_call_target="tpu_custom_call" | custom-call | flops 251658240 | bytes 983040 | tf_op jit(solution)/shard_map/chi_freq/pallas_call | solution.py:277
  54.4 5.2 %all-to-all-done.2.message_ref = f32[8,2,128]{2,1,0:T(2,128)S(1)} async-done(((f32[8,2,128]{2,1,0:T(2,128)}), f32[8,2,128]{2,1,0:T(2,128)S(1)}, u32[]{:S(2)}, u32[]{:S(2)}) %all-to-all-start.2) | async-done | bytes 8224 | tf_op jit(solution)/shard_map/all_to_all | solution.py:307
  59.6 0.9 %forces.1 = f32[3,1000]{1,0:T(4,128)} custom-call(f32[8,2,128]{2,1,0:T(2,128)S(1)} %all-to-all-done.2.message_ref), custom_call_target="tpu_custom_call" | custom-call | tf_op jit(solution)/shard_map/forces/pallas_call | solution.py:308
  (2 shorter events, 0.0 us)
Async XLA Ops:
  2.8 8.5 %copy-start.3 = (f32[3,32]{1,0:T(4,128)S(1)}, f32[3,32]{1,0:T(4,128)}, u32[]{:S(2)}) copy-start(f32[3,32]{1,0:T(4,128)} %param.11) | copy-start | bytes 1156
  2.8 8.6 %copy-start = (bf16[16,32,480]{2,1,0:T(8,128)(2,1)S(1)}, bf16[16,32,480]{2,1,0:T(8,128)(2,1)}, u32[]{:S(2)}) copy-start(bf16[16,32,480]{2,1,0:T(8,128)(2,1)} %adjoint_ref.1) | copy-start | bytes 1474564
  2.8 8.6 %copy-start.1 = (bf16[256,256]{1,0:T(8,128)(2,1)S(1)}, bf16[256,256]{1,0:T(8,128)(2,1)}, u32[]{:S(2)}) copy-start(bf16[256,256]{1,0:T(8,128)(2,1)} %constant.5.clone.high_ref) | copy-start | bytes 393220
  2.8 8.6 %copy-start.2 = (bf16[256,256]{1,0:T(8,128)(2,1)S(1)}, bf16[256,256]{1,0:T(8,128)(2,1)}, u32[]{:S(2)}) copy-start(bf16[256,256]{1,0:T(8,128)(2,1)} %constant.6.clone.low_ref) | copy-start | bytes 393220
  2.8 21.7 %all-to-all-start = ((bf16[8,240,128]{2,1,0:T(8,128)(2,1)}), bf16[8,240,128]{2,1,0:T(8,128)(2,1)S(1)}, u32[]{:S(2)}, u32[]{:S(2)}) async-start(bf16[8,240,128]{2,1,0:T(8,128)(2,1)} %product.1), calls=%async_computation | async-start | bytes 983040 | tf_op jit(solution)/shard_map/all_to_all | solution.py:273
  43.0 16.6 %all-to-all-start.2 = ((f32[8,2,128]{2,1,0:T(2,128)}), f32[8,2,128]{2,1,0:T(2,128)S(1)}, u32[]{:S(2)}, u32[]{:S(2)}) async-start(f32[8,2,128]{2,1,0:T(2,128)} %broadcast_in_dim.16), calls=%async_computation.2 | async-start | bytes 16384 | tf_op jit(solution)/shard_map/all_to_all | solution.py:307

commit v5 on v4

--- a/solution.py
+++ b/solution.py
@@ -103,75 +103,9 @@
     return total + jnp.dot(low_ref[...], values, preferred_element_type=jnp.float32)
 
 
-def adjoint_kernel(high_ref, low_ref, adjoint_ref, out_ref):
-    n_freq, rows, width = adjoint_ref.shape
-    n_source = out_ref.shape[0]
-    per_source, halves = n_freq // n_source, rows // GROUP
-    n_block = per_source * halves
-    head, hole = own_place()
-    split = LANES - head * SHIFT
-    quarter = lax.broadcasted_iota(jnp.int32, (GROUP, LANES), 1) // SHIFT
-    wide = lax.broadcasted_iota(jnp.int32, (n_freq * GROUP, LANES), 1)
-    rests = {}
-    for half in range(halves):
-        block = pl.ds(half * GROUP, GROUP)
-        values = adjoint_ref[:, block, :].reshape(n_freq * GROUP, width)
-        total = transformed(high_ref, low_ref, values)
-        pad = jnp.zeros((n_freq * GROUP, (FULL + 1) * LANES - width), jnp.float32)
-        total = jnp.concatenate([total, pad], axis=1)
-        turned = [
-            pltpu.roll(total[:, m * LANES : (m + 1) * LANES], lax.rem(split, LANES), 1)
-            for m in range(FULL + 1)
-        ]
-        packed = [jnp.where(wide < split, turned[m], turned[m + 1]) for m in range(FULL)]
-        rest = jnp.where(wide < split, turned[FULL], turned[0])
-        for t in range(n_freq):
-            i, tt = divmod(t, per_source)
-            q = tt * halves + half
-            lines = slice(t * GROUP, (t + 1) * GROUP)
-            for m in range(FULL):
-                out_ref[i, pl.ds((q * FULL + m) * GROUP, GROUP), :] = packed[m][lines]
-            rests[i, q] = rest[lines]
-    for i in range(n_source):
-        for m in range(FULL):
-            moved = pltpu.roll(rests[i, n_block - 1], LANES - (1 + m) * SHIFT, 1)
-            filled = jnp.where(quarter == hole, moved, rests[i, m])
-            out_ref[i, pl.ds((n_block * FULL + m) * GROUP, GROUP), :] = filled
-
-
-def energy_kernel(rows, times_ref, adjoint_ref, weight_ref, label_ref, message_ref):
-    n_source, lines, _ = times_ref.shape
-    n_block = lines // GROUP // FULL - 1
-    halves = rows // GROUP
-    _, hole = own_place()
-    in_hole = lax.broadcasted_iota(jnp.int32, (GROUP, LANES), 1) // SHIFT == hole
-    sums = [jnp.zeros((GROUP, LANES), jnp.float32) for _ in range(halves)]
-
-    def terms(tile):
-        lines = pl.ds(tile * GROUP, GROUP)
-        total = jnp.zeros((GROUP, LANES), jnp.float32)
-        for i in range(n_source):
-            total += times_ref[i, lines, :].astype(jnp.float32) * adjoint_ref[i, lines, :]
-        return total
-
-    for q in range(n_block):
-        for m in range(FULL):
-            sums[q % halves] += terms(q * FULL + m)
-    for m in range(FULL):
-        rest = terms(n_block * FULL + m)
-        sums[m % halves] += jnp.where(in_hole, 0.0, rest)
-        sums[(n_block - 1) % halves] += jnp.where(in_hole, rest, 0.0)
-    total = jnp.zeros((1, LANES), jnp.float32)
-    for half in range(halves):
-        energy = jnp.sum(sums[half], axis=1, keepdims=True)
-        row = lax.broadcasted_iota(jnp.int32, (GROUP, LANES), 0) + half * GROUP
-        lane = lax.broadcasted_iota(jnp.int32, (GROUP, LANES), 1)
-        total += jnp.sum(jnp.where(lane % rows == row, energy, 0.0), axis=0, keepdims=True)
-    message = total * weight_ref[...] + label_ref[...]
-    message_ref[...] = jnp.broadcast_to(message, message_ref.shape)
-
-
-def chi_kernel(high_ref, low_ref, times_ref, chi_ref):
+def transform_kernel(
+    high_ref, low_ref, times_ref, adjoint_ref, weight_ref, label_ref, chi_ref, message_ref
+):
     n_source = times_ref.shape[0]
     n_freq, rows, width = chi_ref.shape
     head, hole = own_place()
@@ -203,19 +137,32 @@
                 parts.append(last_rest(i))
         return jnp.concatenate(parts, axis=0)
 
+    total = jnp.zeros((1, LANES), jnp.float32)
     for half in range(rows // GROUP):
         block = pl.ds(half * GROUP, GROUP)
         values = jnp.concatenate([column_tile(half, m) for m in range(FULL + 1)], axis=1)
         chi = transformed(high_ref, low_ref, values)
         turned = [pltpu.roll(chi[:, m * LANES : (m + 1) * LANES], turn, 1) for m in range(FULL + 1)]
+        energy = jnp.zeros((GROUP, 1), jnp.float32)
         for m in range(FULL + 1):
+            before = turned[m - 1]
             count = min(LANES, width - m * LANES)
-            natural = jnp.where(wide < turn, turned[m - 1], turned[m])[:, :count]
-            natural = natural.astype(jnp.bfloat16).reshape(n_freq, GROUP, count)
-            chi_ref[:, block, pl.ds(m * LANES, count)] = natural
-
-
-def forces_kernel(rows, n_col, message_ref, forces_ref):
+            columns = pl.ds(m * LANES, count)
+            natural = jnp.where(wide < turn, before, turned[m])[:, :count].astype(jnp.bfloat16)
+            natural = natural.reshape(n_freq, GROUP, count)
+            chi_ref[:, block, columns] = natural
+            terms = adjoint_ref[:, block, columns].astype(jnp.float32) * natural.astype(jnp.float32)
+            energy += jnp.sum(jnp.sum(terms, axis=0), axis=1, keepdims=True)
+        row = lax.broadcasted_iota(jnp.int32, (GROUP, LANES), 0) + half * GROUP
+        lane = lax.broadcasted_iota(jnp.int32, (GROUP, LANES), 1)
+        total += jnp.sum(jnp.where(lane % rows == row, energy, 0.0), axis=0, keepdims=True)
+    message = total * weight_ref[...] + label_ref[...]
+    message_ref[...] = jnp.broadcast_to(message, message_ref.shape)
+
+
+def forces_kernel(rows, n_col, message_ref, chi_ref, forces_out_ref, chi_out_ref, forces_ref, sems):
+    store = pltpu.make_async_copy(chi_ref, chi_out_ref, sems.at[0])
+    store.start()
     sums = []
     for block in range(message_ref.shape[0] // n_col * CORES):
         pair, core = divmod(block, CORES)
@@ -242,6 +189,10 @@
     for u in range(n_upper):
         count = min(LANES, NATOM - u * LANES)
         forces_ref[:, u * LANES : u * LANES + count] = forces[u * 8 : u * 8 + 3, :count]
+    forces_store = pltpu.make_async_copy(forces_ref, forces_out_ref, sems.at[1])
+    forces_store.start()
+    forces_store.wait()
+    store.wait()
 
 
 def on_device(sizes, green_occ, green_virt, adjoint_w, grad_basis, owner_map, block_offset):
@@ -272,45 +223,38 @@
     )(green_occ, green_virt)
     times = lax.all_to_all(product, "tm", split_axis=0, concat_axis=0, tiled=True)
 
-    def kernel(body, name, shape, dtype, limit, *operands):
-        elements = NTAU * rows * width
-        return pl.pallas_call(
-            body,
-            out_shape=jax.ShapeDtypeStruct(shape, dtype),
-            cost_estimate=pl.CostEstimate(
-                flops=4 * NTAU * GROUP * elements, bytes_accessed=4 * elements, transcendentals=0
-            ),
-            compiler_params=pltpu.CompilerParams(vmem_limit_bytes=limit << 20),
-            name=name,
-        )(*operands)
-
     scale = 1.0 / math.sqrt(NTAU * NG)
     owners = lax.dynamic_slice_in_dim(owner_map, block_offset[0], rows, 0)
     weight = jnp.concatenate([grad_basis.reshape(3 * rows) * scale, jnp.zeros((rows,), jnp.float32)])
     label = jnp.concatenate(
         [jnp.zeros((3 * rows,), jnp.float32), owners.astype(jnp.float32) * (1.0 / (n_col * n_tm))]
     )
-    adjoint = kernel(adjoint_kernel, "adjoint", packed, jnp.float32, 16, high, low, adjoint_w)
-    message = pl.pallas_call(
-        functools.partial(energy_kernel, rows),
-        out_shape=jax.ShapeDtypeStruct((CORES * n_near * n_tm, LANES), jnp.float32),
+    shape = (NTAU, rows, width)
+    chi_freq, message = pl.pallas_call(
+        transform_kernel,
+        out_shape=(
+            pltpu.VMEM(shape, jnp.bfloat16),
+            jax.ShapeDtypeStruct((CORES * n_near * n_tm, LANES), jnp.float32),
+        ),
         compiler_params=pltpu.CompilerParams(vmem_limit_bytes=16 << 20),
-        name="energy",
-    )(times, adjoint, weight[None, :], label[None, :])
+        name="transform",
+    )(high, low, times, adjoint_w, weight[None, :], label[None, :])
 
     message = lax.all_to_all(message, ("core", "near", "tm"), split_axis=0, concat_axis=0, tiled=True)
-    chi_freq = kernel(
-        chi_kernel, "chi_freq", (NTAU, rows, width), jnp.bfloat16, 16, high, low, times
-    )
     message = jnp.sum(message.reshape(CORES, n_near * n_tm, LANES), axis=1)
     message = jnp.broadcast_to(message[None], (n_pair * FAR, CORES, LANES))
     message = lax.all_to_all(message, ("pair", "far"), split_axis=0, concat_axis=0, tiled=True)
-    forces = pl.pallas_call(
+    forces, chi_freq = pl.pallas_call(
         functools.partial(forces_kernel, rows, FAR),
-        out_shape=jax.ShapeDtypeStruct((3, NATOM), jnp.float32),
+        out_specs=[pl.BlockSpec(memory_space=pl.ANY)] * 2,
+        out_shape=(
+            jax.ShapeDtypeStruct((3, NATOM), jnp.float32),
+            jax.ShapeDtypeStruct(shape, jnp.bfloat16),
+        ),
+        scratch_shapes=[pltpu.VMEM((3, NATOM), jnp.float32), pltpu.SemaphoreType.DMA((2,))],
         compiler_params=pltpu.CompilerParams(vmem_limit_bytes=8 << 20),
         name="forces",
-    )(message)
+    )(message, chi_freq)
     return (chi_freq, forces)
 
 

time: 60.8 us -> 60.6 us (level)
  blocking collectives: 17.7 us -> 34 us
  starting transfers between devices: 17.8 us -> 7.79 us
  waiting for transfers between devices: 16.8 us -> 12.3 us
  Pallas kernels: 5.21 us -> 3.81 us
    all_to_all x0 -> x1, blocking collectives: none -> 16.4 us  [on_device(): lax.all_to_all(message, ('pair', 'far'), split_axis=0, concat_axis=0, til...]
    all_to_all x1 -> x0, starting transfers between devices: 10 us -> none  [on_device(): lax.all_to_all(message, ('pair', 'far'), split_axis=0, concat_axis=0, til...]
    all_to_all x1 -> x0, waiting for transfers between devices: 5.21 us -> none  [on_device(): lax.all_to_all(message, ('pair', 'far'), split_axis=0, concat_axis=0, til...]
    pallas_call x4 -> x2, Pallas kernels: 3.06 us -> 1.66 us  [the longest x1 0.92 us: on_device(): pl.pallas_call(functools.partial(forces_kernel, rows, FAR), out_specs=[pl...]
    all_to_all x1, waiting for transfers between devices: 11.6 us -> 12.3 us  [on_device(): lax.all_to_all(product, 'tm', split_axis=0, concat_axis=0, tiled=True)]
  transfers between devices with their start and end apart: 2 -> 1, of which waited for: 2 -> 1; matrix products, arithmetic and copies ran while one was open for 2% -> 2% of each run, Pallas kernels for 3% -> 0%
where the time goes in v5:
time: 60.6 us; the launch traced here: 60.3 us
  blocking collectives  34 us (56%)
  waiting for transfers between devices  12.3 us (20%)
  starting transfers between devices  7.79 us (13%)
  Pallas kernels  3.81 us (6%)
  between operations  1.35 us (2%)
  other arithmetic  0.8 us (1%)
    all_to_all x1, blocking collectives, on_device(): lax.all_to_all(message, ('core', 'near', 'tm'), split_axis=0, concat_axis...  17.7 us
    all_to_all x1, blocking collectives, on_device(): lax.all_to_all(message, ('pair', 'far'), split_axis=0, concat_axis=0, til...  16.4 us
    all_to_all x1, waiting for transfers between devices, on_device(): lax.all_to_all(product, 'tm', split_axis=0, concat_axis=0, tiled=True)  12.3 us
    all_to_all x1, starting transfers between devices, on_device(): lax.all_to_all(product, 'tm', split_axis=0, concat_axis=0, tiled=True)  7.79 us
    pallas_call x1, Pallas kernels, on_device(): pl.pallas_call(product_kernel, in_specs=[pl.BlockSpec(memory_space=pl.ANY...  2.16 us
  transfers between devices with their start and end apart: 1, of which 1 were waited for; matrix products, arithmetic and copies ran while one was open for 2% of the time, Pallas kernels for 0%

profile of v5, /device:TPU:1, one launch (start us, length us, event | category | flops | bytes accessed | tf_op | source)
XLA Modules:
  0.0 60.3 jit_solution(9122872689866934213)
XLA Ops:
  0.6 2.2 %product.1 = bf16[8,240,128]{2,1,0:T(8,128)(2,1)} custom-call(bf16[2,32,3840]{2,1,0:T(8,128)(2,1)} %occ_ref.1, bf16[2,32,3840]{2,1,0:T(8,128)(2,1)} %virt_ref.1), custom_call_target="tpu_custom_call" | custom-call | tf_op jit(solution)/shard_map/product/pallas_call | solution.py:209
  2.8 0.0 copy-start.3
  2.8 0.0 copy-start
  2.8 0.0 copy-start.1
  2.8 0.0 copy-start.2
  2.8 7.8 %all-to-all-start = ((bf16[8,240,128]{2,1,0:T(8,128)(2,1)}), bf16[8,240,128]{2,1,0:T(8,128)(2,1)S(1)}, u32[]{:S(2)}, u32[]{:S(2)}) async-start(bf16[8,240,128]{2,1,0:T(8,128)(2,1)} %product.1), calls=%async_computation | async-start | bytes 983040 | tf_op jit(solution)/shard_map/all_to_all | solution.py:224
  11.3 0.0 copy-done.3
  11.3 0.1 mul.17
  11.4 0.8 %convert_multiply_fusion = f32[32]{0:T(128)S(1)} fusion(s32[30720]{0:T(1024)} %param.12, s32[]{:T(128)S(6)} %select_n.3), kind=kLoop, calls=%fused_computation.3 | loop fusion | flops 64 | bytes 260 | tf_op jit(solution)/shard_map/mul | solution.py:230
  12.2 0.1 pad_bitcast_fusion
  12.2 12.3 %all-to-all-done.times_ref = bf16[8,240,128]{2,1,0:T(8,128)(2,1)S(1)} async-done(((bf16[8,240,128]{2,1,0:T(8,128)(2,1)}), bf16[8,240,128]{2,1,0:T(8,128)(2,1)S(1)}, u32[]{:S(2)}, u32[]{:S(2)}) %all-to-all-start) | async-done | bytes 491552 | tf_op jit(solution)/shard_map/all_to_all | solution.py:224
  24.5 0.0 copy-done
  24.5 0.0 copy-done.1
  24.5 0.0 copy-done.2
  24.5 0.7 %transform.1 = (bf16[16,32,480]{2,1,0:T(8,128)(2,1)S(1)}, f32[64,128]{1,0:T(8,128)S(1)}) custom-call(bf16[256,256]{1,0:T(8,128)(2,1)S(1)} %copy-done.2, bf16[256,256]{1,0:T(8,128)(2,1)S(1)} %copy-done.1, bf16[8,240,128]{2,1,0:T(8,128)(2,1)S(1)} %all-to-all-done.times_ref, bf16[16,32,480]{2,1,0:T(8,128)(2,1)S(1)} %copy-done, ...), custom_call_target="tpu_custom_call" | custom-call | tf_op jit(solution)/shard_map/transform/pallas_call | solution.py:233
  25.3 17.7 %all_to_all.19 = f32[64,1,128]{2,1,0:T(1,128)S(1)} all-to-all(f32[64,1,128]{2,1,0:T(1,128)S(1)} %bitcast.14), channel_id=1, replica_groups=mesh['pair'=4,'core'=2,'near'=4,'far'=2,'tm'=8] {'core','near','tm'}, dimensions={0} | all-to-all | bytes 65536 | tf_op jit(solution)/shard_map/all_to_all | solution.py:243
  43.0 16.4 %all_to_all.20.message_ref = f32[8,2,128]{2,1,0:T(2,128)S(1)} all-to-all(f32[8,2,128]{2,1,0:T(2,128)S(1)} %broadcast_in_dim.16), channel_id=1, replica_groups=mesh['pair'=4,'core'=2,'near'=4,'far'=2,'tm'=8] {'pair','far'}, dimensions={0} | all-to-all | bytes 16384 | tf_op jit(solution)/shard_map/all_to_all | solution.py:246
  59.4 0.9 %forces.1 = (f32[3,1000]{1,0:T(4,128)}, bf16[16,32,480]{2,1,0:T(8,128)(2,1)}) custom-call(f32[8,2,128]{2,1,0:T(2,128)S(1)} %all_to_all.20.message_ref, bf16[16,32,480]{2,1,0:T(8,128)(2,1)S(1)} %get-tuple-element.7.chi_ref), custom_call_target="tpu_custom_call" | custom-call | tf_op jit(solution)/shard_map/forces/pallas_call | solution.py:247
  (3 shorter events, 0.0 us)
Async XLA Ops:
  2.8 8.5 %copy-start.3 = (f32[3,32]{1,0:T(4,128)S(1)}, f32[3,32]{1,0:T(4,128)}, u32[]{:S(2)}) copy-start(f32[3,32]{1,0:T(4,128)} %param.11) | copy-start | bytes 1156
  2.8 21.7 %copy-start = (bf16[16,32,480]{2,1,0:T(8,128)(2,1)S(1)}, bf16[16,32,480]{2,1,0:T(8,128)(2,1)}, u32[]{:S(2)}) copy-start(bf16[16,32,480]{2,1,0:T(8,128)(2,1)} %adjoint_ref.1) | copy-start | bytes 1474564
  2.8 21.7 %copy-start.1 = (bf16[256,256]{1,0:T(8,128)(2,1)S(1)}, bf16[256,256]{1,0:T(8,128)(2,1)}, u32[]{:S(2)}) copy-start(bf16[256,256]{1,0:T(8,128)(2,1)} %constant.6.clone.low_ref) | copy-start | bytes 393220
  2.8 21.7 %copy-start.2 = (bf16[256,256]{1,0:T(8,128)(2,1)S(1)}, bf16[256,256]{1,0:T(8,128)(2,1)}, u32[]{:S(2)}) copy-start(bf16[256,256]{1,0:T(8,128)(2,1)} %constant.5.clone.high_ref) | copy-start | bytes 393220
  2.8 21.7 %all-to-all-start = ((bf16[8,240,128]{2,1,0:T(8,128)(2,1)}), bf16[8,240,128]{2,1,0:T(8,128)(2,1)S(1)}, u32[]{:S(2)}, u32[]{:S(2)}) async-start(bf16[8,240,128]{2,1,0:T(8,128)(2,1)} %product.1), calls=%async_computation | async-start | bytes 983040 | tf_op jit(solution)/shard_map/all_to_all | solution.py:224

commit v6 on v4

--- a/solution.py
+++ b/solution.py
@@ -171,7 +171,7 @@
     message_ref[...] = jnp.broadcast_to(message, message_ref.shape)
 
 
-def chi_kernel(high_ref, low_ref, times_ref, chi_ref):
+def write_chi(high_ref, low_ref, times_ref, chi_ref, done):
     n_source = times_ref.shape[0]
     n_freq, rows, width = chi_ref.shape
     head, hole = own_place()
@@ -213,9 +213,21 @@
             natural = jnp.where(wide < turn, turned[m - 1], turned[m])[:, :count]
             natural = natural.astype(jnp.bfloat16).reshape(n_freq, GROUP, count)
             chi_ref[:, block, pl.ds(m * LANES, count)] = natural
-
-
-def forces_kernel(rows, n_col, message_ref, forces_ref):
+        done(half, block)
+
+
+def forces_kernel(
+    rows, n_col, message_ref, high_ref, low_ref, times_ref,
+    forces_out_ref, chi_out_ref, forces_ref, chi_ref, sems,
+):
+    stores = []
+
+    def send(half, block):
+        store = pltpu.make_async_copy(chi_ref.at[:, block], chi_out_ref.at[:, block], sems.at[half])
+        store.start()
+        stores.append(store)
+
+    write_chi(high_ref, low_ref, times_ref, chi_ref, send)
     sums = []
     for block in range(message_ref.shape[0] // n_col * CORES):
         pair, core = divmod(block, CORES)
@@ -242,6 +254,10 @@
     for u in range(n_upper):
         count = min(LANES, NATOM - u * LANES)
         forces_ref[:, u * LANES : u * LANES + count] = forces[u * 8 : u * 8 + 3, :count]
+    store = pltpu.make_async_copy(forces_ref, forces_out_ref, sems.at[rows // GROUP])
+    store.start()
+    for store in [*stores, store]:
+        store.wait()
 
 
 def on_device(sizes, green_occ, green_virt, adjoint_w, grad_basis, owner_map, block_offset):
@@ -299,18 +315,25 @@
     )(times, adjoint, weight[None, :], label[None, :])
 
     message = lax.all_to_all(message, ("core", "near", "tm"), split_axis=0, concat_axis=0, tiled=True)
-    chi_freq = kernel(
-        chi_kernel, "chi_freq", (NTAU, rows, width), jnp.bfloat16, 16, high, low, times
-    )
     message = jnp.sum(message.reshape(CORES, n_near * n_tm, LANES), axis=1)
     message = jnp.broadcast_to(message[None], (n_pair * FAR, CORES, LANES))
     message = lax.all_to_all(message, ("pair", "far"), split_axis=0, concat_axis=0, tiled=True)
-    forces = pl.pallas_call(
+    shape = (NTAU, rows, width)
+    forces, chi_freq = pl.pallas_call(
         functools.partial(forces_kernel, rows, FAR),
-        out_shape=jax.ShapeDtypeStruct((3, NATOM), jnp.float32),
-        compiler_params=pltpu.CompilerParams(vmem_limit_bytes=8 << 20),
+        out_specs=[pl.BlockSpec(memory_space=pl.ANY)] * 2,
+        out_shape=(
+            jax.ShapeDtypeStruct((3, NATOM), jnp.float32),
+            jax.ShapeDtypeStruct(shape, jnp.bfloat16),
+        ),
+        scratch_shapes=[
+            pltpu.VMEM((3, NATOM), jnp.float32),
+            pltpu.VMEM(shape, jnp.bfloat16),
+            pltpu.SemaphoreType.DMA((rows // GROUP + 1,)),
+        ],
+        compiler_params=pltpu.CompilerParams(vmem_limit_bytes=16 << 20),
         name="forces",
-    )(message)
+    )(message, high, low, times)
     return (chi_freq, forces)
 
 

time: 60.8 us -> 60.4 us (level)
  blocking collectives: 17.7 us -> 34 us
  starting transfers between devices: 17.8 us -> 7.79 us
  waiting for transfers between devices: 16.8 us -> 11.6 us
  Pallas kernels: 5.21 us -> 4.29 us
    all_to_all x0 -> x1, blocking collectives: none -> 16.4 us  [on_device(): lax.all_to_all(message, ('pair', 'far'), split_axis=0, concat_axis=0, til...]
    all_to_all x1 -> x0, starting transfers between devices: 10 us -> none  [on_device(): lax.all_to_all(message, ('pair', 'far'), split_axis=0, concat_axis=0, til...]
    all_to_all x1 -> x0, waiting for transfers between devices: 5.21 us -> none  [on_device(): lax.all_to_all(message, ('pair', 'far'), split_axis=0, concat_axis=0, til...]
    pallas_call x2 -> x1, Pallas kernels: 1.96 us -> 0.65 us  [kernel(): pl.pallas_call(body, out_shape=jax.ShapeDtypeStruct(shape, dtype), cost_e...]
  transfers between devices with their start and end apart: 2 -> 1, of which waited for: 2 -> 1; matrix products, arithmetic and copies ran while one was open for 2% -> 2% of each run, Pallas kernels for 3% -> 1%
where the time goes in v6:
time: 60.4 us; the launch traced here: 60.1 us
  blocking collectives  34 us (56%)
  waiting for transfers between devices  11.6 us (19%)
  starting transfers between devices  7.79 us (13%)
  Pallas kernels  4.29 us (7%)
  between operations  1.34 us (2%)
  other arithmetic  0.8 us (1%)
    all_to_all x1, blocking collectives, on_device(): lax.all_to_all(message, ('core', 'near', 'tm'), split_axis=0, concat_axis...  17.7 us
    all_to_all x1, blocking collectives, on_device(): lax.all_to_all(message, ('pair', 'far'), split_axis=0, concat_axis=0, til...  16.4 us
    all_to_all x1, waiting for transfers between devices, on_device(): lax.all_to_all(product, 'tm', split_axis=0, concat_axis=0, tiled=True)  11.6 us
    all_to_all x1, starting transfers between devices, on_device(): lax.all_to_all(product, 'tm', split_axis=0, concat_axis=0, tiled=True)  7.79 us
    pallas_call x1, Pallas kernels, on_device(): pl.pallas_call(product_kernel, in_specs=[pl.BlockSpec(memory_space=pl.ANY...  2.16 us
    pallas_call x1, Pallas kernels, on_device(): pl.pallas_call(functools.partial(forces_kernel, rows, FAR), out_specs=[pl...  1.29 us
  transfers between devices with their start and end apart: 1, of which 1 were waited for; matrix products, arithmetic and copies ran while one was open for 2% of the time, Pallas kernels for 1%

profile of v6, /device:TPU:1, one launch (start us, length us, event | category | flops | bytes accessed | tf_op | source)
XLA Modules:
  0.0 60.1 jit_solution(4086250167056549364)
XLA Ops:
  0.6 2.2 %product.1 = bf16[8,240,128]{2,1,0:T(8,128)(2,1)} custom-call(bf16[2,32,3840]{2,1,0:T(8,128)(2,1)} %occ_ref.1, bf16[2,32,3840]{2,1,0:T(8,128)(2,1)} %virt_ref.1), custom_call_target="tpu_custom_call" | custom-call | tf_op jit(solution)/shard_map/product/pallas_call | solution.py:274
  2.8 0.0 copy-start.3
  2.8 0.0 copy-start
  2.8 0.0 copy-start.1
  2.8 0.0 copy-start.2
  2.8 7.8 %all-to-all-start = ((bf16[8,240,128]{2,1,0:T(8,128)(2,1)}), bf16[8,240,128]{2,1,0:T(8,128)(2,1)S(1)}, u32[]{:S(2)}, u32[]{:S(2)}) async-start(bf16[8,240,128]{2,1,0:T(8,128)(2,1)} %product.1), calls=%async_computation | async-start | bytes 983040 | tf_op jit(solution)/shard_map/all_to_all | solution.py:289
  11.3 0.0 copy-done.3
  11.3 0.1 mul.17
  11.4 0.0 copy-done
  11.4 0.0 copy-done.1
  11.4 0.0 copy-done.2
  11.4 0.6 %adjoint.1.adjoint_ref = f32[8,240,128]{2,1,0:T(8,128)S(1)} custom-call(bf16[256,256]{1,0:T(8,128)(2,1)S(1)} %copy-done.2, bf16[256,256]{1,0:T(8,128)(2,1)S(1)} %copy-done.1, bf16[16,32,480]{2,1,0:T(8,128)(2,1)S(1)} %copy-done), custom_call_target="tpu_custom_call" | custom-call | flops 251658240 | bytes 983040 | tf_op jit(solution)/shard_map/adjoint/pallas_call | solution.py:293
  12.0 0.8 %convert_multiply_fusion = f32[32]{0:T(128)S(1)} fusion(s32[30720]{0:T(1024)} %param.12, s32[]{:T(128)S(6)} %select_n.3), kind=kLoop, calls=%fused_computation.3 | loop fusion | flops 64 | bytes 260 | tf_op jit(solution)/shard_map/mul | solution.py:307
  12.8 0.1 pad_bitcast_fusion
  12.9 11.6 %all-to-all-done.times_ref = bf16[8,240,128]{2,1,0:T(8,128)(2,1)S(1)} async-done(((bf16[8,240,128]{2,1,0:T(8,128)(2,1)}), bf16[8,240,128]{2,1,0:T(8,128)(2,1)S(1)}, u32[]{:S(2)}, u32[]{:S(2)}) %all-to-all-start) | async-done | bytes 491552 | tf_op jit(solution)/shard_map/all_to_all | solution.py:289
  24.5 0.2 energy.1
  24.7 17.7 %all_to_all.19 = f32[64,1,128]{2,1,0:T(1,128)S(1)} all-to-all(f32[64,1,128]{2,1,0:T(1,128)S(1)} %bitcast.14), channel_id=1, replica_groups=mesh['pair'=4,'core'=2,'near'=4,'far'=2,'tm'=8] {'core','near','tm'}, dimensions={0} | all-to-all | bytes 65536 | tf_op jit(solution)/shard_map/all_to_all | solution.py:317
  42.4 16.4 %all_to_all.20.message_ref = f32[8,2,128]{2,1,0:T(2,128)S(1)} all-to-all(f32[8,2,128]{2,1,0:T(2,128)S(1)} %broadcast_in_dim.16), channel_id=1, replica_groups=mesh['pair'=4,'core'=2,'near'=4,'far'=2,'tm'=8] {'pair','far'}, dimensions={0} | all-to-all | bytes 16384 | tf_op jit(solution)/shard_map/all_to_all | solution.py:320
  58.8 1.3 %forces.1 = (f32[3,1000]{1,0:T(4,128)}, bf16[16,32,480]{2,1,0:T(8,128)(2,1)}) custom-call(f32[8,2,128]{2,1,0:T(2,128)S(1)} %all_to_all.20.message_ref, bf16[256,256]{1,0:T(8,128)(2,1)S(1)} %copy-done.2, bf16[256,256]{1,0:T(8,128)(2,1)S(1)} %copy-done.1, bf16[8,240,128]{2,1,0:T(8,128)(2,1)S(1)} %all-to-all-done.times_ref), custom_call_target="tpu_custom_call" | custom-call | tf_op jit(solution)/shard_map/forces/pallas_call | solution.py:322
  (3 shorter events, 0.0 us)
Async XLA Ops:
  2.8 8.5 %copy-start.3 = (f32[3,32]{1,0:T(4,128)S(1)}, f32[3,32]{1,0:T(4,128)}, u32[]{:S(2)}) copy-start(f32[3,32]{1,0:T(4,128)} %param.11) | copy-start | bytes 1156
  2.8 8.6 %copy-start = (bf16[16,32,480]{2,1,0:T(8,128)(2,1)S(1)}, bf16[16,32,480]{2,1,0:T(8,128)(2,1)}, u32[]{:S(2)}) copy-start(bf16[16,32,480]{2,1,0:T(8,128)(2,1)} %adjoint_ref.1) | copy-start | bytes 1474564
  2.8 8.6 %copy-start.1 = (bf16[256,256]{1,0:T(8,128)(2,1)S(1)}, bf16[256,256]{1,0:T(8,128)(2,1)}, u32[]{:S(2)}) copy-start(bf16[256,256]{1,0:T(8,128)(2,1)} %constant.6.clone.low_ref) | copy-start | bytes 393220
  2.8 8.6 %copy-start.2 = (bf16[256,256]{1,0:T(8,128)(2,1)S(1)}, bf16[256,256]{1,0:T(8,128)(2,1)}, u32[]{:S(2)}) copy-start(bf16[256,256]{1,0:T(8,128)(2,1)} %constant.5.clone.high_ref) | copy-start | bytes 393220
  2.8 21.7 %all-to-all-start = ((bf16[8,240,128]{2,1,0:T(8,128)(2,1)}), bf16[8,240,128]{2,1,0:T(8,128)(2,1)S(1)}, u32[]{:S(2)}, u32[]{:S(2)}) async-start(bf16[8,240,128]{2,1,0:T(8,128)(2,1)} %product.1), calls=%async_computation | async-start | bytes 983040 | tf_op jit(solution)/shard_map/all_to_all | solution.py:289

commit v7 on v6

--- a/solution.py
+++ b/solution.py
@@ -228,29 +228,52 @@
         stores.append(store)
 
     write_chi(high_ref, low_ref, times_ref, chi_ref, send)
+    n_pair = message_ref.shape[0] // n_col
     sums = []
-    for block in range(message_ref.shape[0] // n_col * CORES):
-        pair, core = divmod(block, CORES)
-        devices = pl.ds(pair * n_col, n_col)
-        sums.append(jnp.sum(message_ref[devices, core, :], axis=0, keepdims=True))
-    parts = [
-        jnp.concatenate([total[:, p * rows : (p + 1) * rows] for total in sums], axis=1)
-        for p in range(4)
-    ]
-    owners = parts[3].astype(jnp.int32)
-    weights = jnp.concatenate(parts[:3] + [jnp.zeros_like(parts[0])] * 5, axis=0)
+    for pair in range(n_pair):
+        total = message_ref[pair * n_col]
+        for i in range(1, n_col):
+            total += message_ref[pair * n_col + i]
+        sums.append(total)
+    sums = jnp.concatenate(sums, axis=0)
+    n_block = n_pair * CORES
+    block = lax.broadcasted_iota(jnp.int32, (n_block, LANES), 0)
+    quarter = lax.broadcasted_iota(jnp.int32, (n_block, LANES), 1) // rows
+    own = quarter == block % QUARTERS
+    turned = [sums if d == 0 else pltpu.roll(sums, d * rows, 1) for d in range(QUARTERS)]
+
+    def along_lanes(part):
+        placed = jnp.zeros((n_block, LANES), jnp.float32)
+        for d in range(QUARTERS):
+            placed = jnp.where(own & (quarter == (part + d) % QUARTERS), turned[d], placed)
+        tiles = [
+            jnp.sum(jnp.where(block // QUARTERS == tile, placed, 0.0), axis=0, keepdims=True)
+            for tile in range(n_block // QUARTERS)
+        ]
+        return jnp.concatenate(tiles, axis=1)
+
+    owners = along_lanes(3).astype(jnp.int32)
+    width = n_block * rows
+    part = lax.broadcasted_iota(jnp.int32, (8, width), 0)
+    weights = jnp.zeros((8, width), jnp.float32)
+    for p in range(3):
+        weights = jnp.where(part == p, along_lanes(p), weights)
     upper, lower = owners // LANES, owners % LANES
     n_upper = pl.cdiv(NATOM, LANES)
-    rest = jnp.concatenate([jnp.where(upper == u, weights, 0.0) for u in range(n_upper)], axis=0)
-    lanes = lax.broadcasted_iota(jnp.int32, (LANES, owners.shape[1]), 0)
+    lanes = lax.broadcasted_iota(jnp.int32, (LANES, width), 0)
     onehot = jnp.where(lanes == lower, 1.0, 0.0).astype(jnp.bfloat16)
-    forces = jnp.zeros((8 * n_upper, LANES), jnp.float32)
+    pieces = []
+    rest = weights
     for _ in range(3):
-        part = rest.astype(jnp.bfloat16)
-        rest = rest - part.astype(jnp.float32)
-        forces += lax.dot_general(
-            part, onehot, (((1,), (1,)), ((), ())), preferred_element_type=jnp.float32
-        )
+        piece = rest.astype(jnp.bfloat16).astype(jnp.float32)
+        rest = rest - piece
+        pieces += [jnp.where(upper == u, piece, 0.0) for u in range(n_upper)]
+    pieces = jnp.concatenate(pieces, axis=0).astype(jnp.bfloat16)
+    products = lax.dot_general(
+        pieces, onehot, (((1,), (1,)), ((), ())), preferred_element_type=jnp.float32
+    )
+    count = 8 * n_upper
+    forces = products[:count] + products[count : 2 * count] + products[2 * count :]
     for u in range(n_upper):
         count = min(LANES, NATOM - u * LANES)
         forces_ref[:, u * LANES : u * LANES + count] = forces[u * 8 : u * 8 + 3, :count]

time: 60.4 us -> 60.4 us (level)
  no operation moved by 1% of the time
where the time goes in v7:
time: 60.4 us; the launch traced here: 60 us
  blocking collectives  34 us (56%)
  waiting for transfers between devices  11.6 us (19%)
  starting transfers between devices  7.79 us (13%)
  Pallas kernels  4.25 us (7%)
  between operations  1.34 us (2%)
  other arithmetic  0.8 us (1%)
    all_to_all x1, blocking collectives, on_device(): lax.all_to_all(message, ('core', 'near', 'tm'), split_axis=0, concat_axis...  17.7 us
    all_to_all x1, blocking collectives, on_device(): lax.all_to_all(message, ('pair', 'far'), split_axis=0, concat_axis=0, til...  16.4 us
    all_to_all x1, waiting for transfers between devices, on_device(): lax.all_to_all(product, 'tm', split_axis=0, concat_axis=0, tiled=True)  11.6 us
    all_to_all x1, starting transfers between devices, on_device(): lax.all_to_all(product, 'tm', split_axis=0, concat_axis=0, tiled=True)  7.79 us
    pallas_call x1, Pallas kernels, on_device(): pl.pallas_call(product_kernel, in_specs=[pl.BlockSpec(memory_space=pl.ANY...  2.16 us
    pallas_call x1, Pallas kernels, on_device(): pl.pallas_call(functools.partial(forces_kernel, rows, FAR), out_specs=[pl...  1.25 us
  transfers between devices with their start and end apart: 1, of which 1 were waited for; matrix products, arithmetic and copies ran while one was open for 2% of the time, Pallas kernels for 1%

profile of v7, /device:TPU:1, one launch (start us, length us, event | category | flops | bytes accessed | tf_op | source)
XLA Modules:
  0.0 60.0 jit_solution(6340235330682701919)
XLA Ops:
  0.6 2.2 %product.1 = bf16[8,240,128]{2,1,0:T(8,128)(2,1)} custom-call(bf16[2,32,3840]{2,1,0:T(8,128)(2,1)} %occ_ref.1, bf16[2,32,3840]{2,1,0:T(8,128)(2,1)} %virt_ref.1), custom_call_target="tpu_custom_call" | custom-call | tf_op jit(solution)/shard_map/product/pallas_call | solution.py:297
  2.8 0.0 copy-start.3
  2.8 0.0 copy-start
  2.8 0.0 copy-start.1
  2.8 0.0 copy-start.2
  2.8 7.8 %all-to-all-start = ((bf16[8,240,128]{2,1,0:T(8,128)(2,1)}), bf16[8,240,128]{2,1,0:T(8,128)(2,1)S(1)}, u32[]{:S(2)}, u32[]{:S(2)}) async-start(bf16[8,240,128]{2,1,0:T(8,128)(2,1)} %product.1), calls=%async_computation | async-start | bytes 983040 | tf_op jit(solution)/shard_map/all_to_all | solution.py:312
  11.3 0.0 copy-done.3
  11.3 0.1 mul.17
  11.4 0.0 copy-done
  11.4 0.0 copy-done.1
  11.4 0.0 copy-done.2
  11.4 0.6 %adjoint.1.adjoint_ref = f32[8,240,128]{2,1,0:T(8,128)S(1)} custom-call(bf16[256,256]{1,0:T(8,128)(2,1)S(1)} %copy-done.2, bf16[256,256]{1,0:T(8,128)(2,1)S(1)} %copy-done.1, bf16[16,32,480]{2,1,0:T(8,128)(2,1)S(1)} %copy-done), custom_call_target="tpu_custom_call" | custom-call | flops 251658240 | bytes 983040 | tf_op jit(solution)/shard_map/adjoint/pallas_call | solution.py:316
  12.0 0.8 %convert_multiply_fusion = f32[32]{0:T(128)S(1)} fusion(s32[30720]{0:T(1024)} %param.12, s32[]{:T(128)S(6)} %select_n.3), kind=kLoop, calls=%fused_computation.3 | loop fusion | flops 64 | bytes 260 | tf_op jit(solution)/shard_map/mul | solution.py:330
  12.8 0.1 pad_bitcast_fusion
  12.9 11.6 %all-to-all-done.times_ref = bf16[8,240,128]{2,1,0:T(8,128)(2,1)S(1)} async-done(((bf16[8,240,128]{2,1,0:T(8,128)(2,1)}), bf16[8,240,128]{2,1,0:T(8,128)(2,1)S(1)}, u32[]{:S(2)}, u32[]{:S(2)}) %all-to-all-start) | async-done | bytes 491552 | tf_op jit(solution)/shard_map/all_to_all | solution.py:312
  24.5 0.2 energy.1
  24.7 17.7 %all_to_all.19 = f32[64,1,128]{2,1,0:T(1,128)S(1)} all-to-all(f32[64,1,128]{2,1,0:T(1,128)S(1)} %bitcast.14), channel_id=1, replica_groups=mesh['pair'=4,'core'=2,'near'=4,'far'=2,'tm'=8] {'core','near','tm'}, dimensions={0} | all-to-all | bytes 65536 | tf_op jit(solution)/shard_map/all_to_all | solution.py:340
  42.4 16.4 %all_to_all.20.message_ref = f32[8,2,128]{2,1,0:T(2,128)S(1)} all-to-all(f32[8,2,128]{2,1,0:T(2,128)S(1)} %broadcast_in_dim.16), channel_id=1, replica_groups=mesh['pair'=4,'core'=2,'near'=4,'far'=2,'tm'=8] {'pair','far'}, dimensions={0} | all-to-all | bytes 16384 | tf_op jit(solution)/shard_map/all_to_all | solution.py:343
  58.8 1.3 %forces.1 = (f32[3,1000]{1,0:T(4,128)}, bf16[16,32,480]{2,1,0:T(8,128)(2,1)}) custom-call(f32[8,2,128]{2,1,0:T(2,128)S(1)} %all_to_all.20.message_ref, bf16[256,256]{1,0:T(8,128)(2,1)S(1)} %copy-done.2, bf16[256,256]{1,0:T(8,128)(2,1)S(1)} %copy-done.1, bf16[8,240,128]{2,1,0:T(8,128)(2,1)S(1)} %all-to-all-done.times_ref), custom_call_target="tpu_custom_call" | custom-call | tf_op jit(solution)/shard_map/forces/pallas_call | solution.py:345
  (3 shorter events, 0.0 us)
Async XLA Ops:
  2.8 8.5 %copy-start.3 = (f32[3,32]{1,0:T(4,128)S(1)}, f32[3,32]{1,0:T(4,128)}, u32[]{:S(2)}) copy-start(f32[3,32]{1,0:T(4,128)} %param.11) | copy-start | bytes 1156
  2.8 8.6 %copy-start = (bf16[16,32,480]{2,1,0:T(8,128)(2,1)S(1)}, bf16[16,32,480]{2,1,0:T(8,128)(2,1)}, u32[]{:S(2)}) copy-start(bf16[16,32,480]{2,1,0:T(8,128)(2,1)} %adjoint_ref.1) | copy-start | bytes 1474564
  2.8 8.6 %copy-start.1 = (bf16[256,256]{1,0:T(8,128)(2,1)S(1)}, bf16[256,256]{1,0:T(8,128)(2,1)}, u32[]{:S(2)}) copy-start(bf16[256,256]{1,0:T(8,128)(2,1)} %constant.6.clone.low_ref) | copy-start | bytes 393220
  2.8 8.6 %copy-start.2 = (bf16[256,256]{1,0:T(8,128)(2,1)S(1)}, bf16[256,256]{1,0:T(8,128)(2,1)}, u32[]{:S(2)}) copy-start(bf16[256,256]{1,0:T(8,128)(2,1)} %constant.5.clone.high_ref) | copy-start | bytes 393220
  2.8 21.7 %all-to-all-start = ((bf16[8,240,128]{2,1,0:T(8,128)(2,1)}), bf16[8,240,128]{2,1,0:T(8,128)(2,1)S(1)}, u32[]{:S(2)}, u32[]{:S(2)}) async-start(bf16[8,240,128]{2,1,0:T(8,128)(2,1)} %product.1), calls=%async_computation | async-start | bytes 983040 | tf_op jit(solution)/shard_map/all_to_all | solution.py:312

commit v8 on v7

--- a/solution.py
+++ b/solution.py
@@ -18,6 +18,7 @@
 SHIFT = 32
 QUARTERS = LANES // SHIFT
 FULL = 3
+ORDER = (0, 2, 4, 6, 1, 3, 5, 7)
 CORES = 2
 FAR = 2
 
@@ -71,7 +72,7 @@
             hole = QUARTERS - 1 - head
             first = (start + head) // QUARTERS
             for m in range(FULL):
-                out[j, pl.ds((q * FULL + m) * GROUP, GROUP), :] = tile(first + m)
+                out[ORDER.index(j), pl.ds((q * FULL + m) * GROUP, GROUP), :] = tile(first + m)
             if head == 0:
                 rest = tile(first + FULL)
             elif hole == 0:
@@ -87,7 +88,7 @@
             for m in range(FULL):
                 moved = roll(rests[j, q], LANES - (1 + m) * SHIFT)
                 filled = jnp.where(quarter == hole, moved, rests[j, m])
-                out[j, pl.ds(((q + 1) * FULL + m) * GROUP, GROUP), :] = filled
+                out[ORDER.index(j), pl.ds(((q + 1) * FULL + m) * GROUP, GROUP), :] = filled
         send(q, q * FULL, 2 * FULL)
     for store in stores:
         store.wait()
@@ -130,13 +131,13 @@
             q = tt * halves + half
             lines = slice(t * GROUP, (t + 1) * GROUP)
             for m in range(FULL):
-                out_ref[i, pl.ds((q * FULL + m) * GROUP, GROUP), :] = packed[m][lines]
+                out_ref[ORDER.index(i), pl.ds((q * FULL + m) * GROUP, GROUP), :] = packed[m][lines]
             rests[i, q] = rest[lines]
     for i in range(n_source):
         for m in range(FULL):
             moved = pltpu.roll(rests[i, n_block - 1], LANES - (1 + m) * SHIFT, 1)
             filled = jnp.where(quarter == hole, moved, rests[i, m])
-            out_ref[i, pl.ds((n_block * FULL + m) * GROUP, GROUP), :] = filled
+            out_ref[ORDER.index(i), pl.ds((n_block * FULL + m) * GROUP, GROUP), :] = filled
 
 
 def energy_kernel(rows, times_ref, adjoint_ref, weight_ref, label_ref, message_ref):
@@ -181,7 +182,7 @@
     n_block = NTAU // n_source * (rows // GROUP)
 
     def stored(i, tile):
-        return times_ref[i, pl.ds(tile * GROUP, GROUP), :]
+        return times_ref[ORDER.index(i), pl.ds(tile * GROUP, GROUP), :]
 
     def last_rest(i):
         rest = stored(i, n_block * FULL)
@@ -309,7 +310,9 @@
         compiler_params=pltpu.CompilerParams(vmem_limit_bytes=60 << 20),
         name="product",
     )(green_occ, green_virt)
-    times = lax.all_to_all(product, "tm", split_axis=0, concat_axis=0, tiled=True)
+    times = lax.all_to_all(
+        product, "tm", split_axis=0, concat_axis=0, tiled=True, axis_index_groups=[ORDER]
+    )
 
     def kernel(body, name, shape, dtype, limit, *operands):
         elements = NTAU * rows * width

time: 60.4 us -> 60.4 us (level)
  no operation moved by 1% of the time
where the time goes in v8:
time: 60.4 us; the launch traced here: 60 us
  blocking collectives  34.6 us (57%)
  waiting for transfers between devices  11 us (18%)
  starting transfers between devices  7.79 us (13%)
  Pallas kernels  4.24 us (7%)
  between operations  1.34 us (2%)
  other arithmetic  0.8 us (1%)
    all_to_all x1, blocking collectives, on_device(): lax.all_to_all(message, ('core', 'near', 'tm'), split_axis=0, concat_axis...  18.3 us
    all_to_all x1, blocking collectives, on_device(): lax.all_to_all(message, ('pair', 'far'), split_axis=0, concat_axis=0, til...  16.4 us
    all_to_all x1, waiting for transfers between devices, on_device(): lax.all_to_all(product, 'tm', split_axis=0, concat_axis=0, tiled=True, ax...  11 us
    all_to_all x1, starting transfers between devices, on_device(): lax.all_to_all(product, 'tm', split_axis=0, concat_axis=0, tiled=True, ax...  7.79 us
    pallas_call x1, Pallas kernels, on_device(): pl.pallas_call(product_kernel, in_specs=[pl.BlockSpec(memory_space=pl.ANY...  2.16 us
    pallas_call x1, Pallas kernels, on_device(): pl.pallas_call(functools.partial(forces_kernel, rows, FAR), out_specs=[pl...  1.25 us
  transfers between devices with their start and end apart: 1, of which 1 were waited for; matrix products, arithmetic and copies ran while one was open for 2% of the time, Pallas kernels for 1%

profile of v8, /device:TPU:1, one launch (start us, length us, event | category | flops | bytes accessed | tf_op | source)
XLA Modules:
  0.0 60.0 jit_solution(9666303927226376349)
XLA Ops:
  0.6 2.2 %product.1 = bf16[8,240,128]{2,1,0:T(8,128)(2,1)} custom-call(bf16[2,32,3840]{2,1,0:T(8,128)(2,1)} %occ_ref.1, bf16[2,32,3840]{2,1,0:T(8,128)(2,1)} %virt_ref.1), custom_call_target="tpu_custom_call" | custom-call | tf_op jit(solution)/shard_map/product/pallas_call | solution.py:298
  2.8 0.0 copy-start.3
  2.8 0.0 copy-start
  2.8 0.0 copy-start.1
  2.8 0.0 copy-start.2
  2.8 7.8 %all-to-all-start = ((bf16[8,240,128]{2,1,0:T(8,128)(2,1)}), bf16[8,240,128]{2,1,0:T(8,128)(2,1)S(1)}, u32[]{:S(2)}, u32[]{:S(2)}) async-start(bf16[8,240,128]{2,1,0:T(8,128)(2,1)} %product.1), calls=%async_computation | async-start | bytes 983040 | tf_op jit(solution)/shard_map/all_to_all | solution.py:313
  11.3 0.0 copy-done.3
  11.3 0.1 mul.17
  11.4 0.0 copy-done
  11.4 0.0 copy-done.1
  11.4 0.0 copy-done.2
  11.4 0.6 %adjoint.1.adjoint_ref = f32[8,240,128]{2,1,0:T(8,128)S(1)} custom-call(bf16[256,256]{1,0:T(8,128)(2,1)S(1)} %copy-done.2, bf16[256,256]{1,0:T(8,128)(2,1)S(1)} %copy-done.1, bf16[16,32,480]{2,1,0:T(8,128)(2,1)S(1)} %copy-done), custom_call_target="tpu_custom_call" | custom-call | flops 251658240 | bytes 983040 | tf_op jit(solution)/shard_map/adjoint/pallas_call | solution.py:319
  12.0 0.8 %convert_multiply_fusion = f32[32]{0:T(128)S(1)} fusion(s32[30720]{0:T(1024)} %param.12, s32[]{:T(128)S(6)} %select_n.3), kind=kLoop, calls=%fused_computation.3 | loop fusion | flops 64 | bytes 260 | tf_op jit(solution)/shard_map/mul | solution.py:333
  12.8 0.1 pad_bitcast_fusion
  12.9 11.0 %all-to-all-done.times_ref = bf16[8,240,128]{2,1,0:T(8,128)(2,1)S(1)} async-done(((bf16[8,240,128]{2,1,0:T(8,128)(2,1)}), bf16[8,240,128]{2,1,0:T(8,128)(2,1)S(1)}, u32[]{:S(2)}, u32[]{:S(2)}) %all-to-all-start) | async-done | bytes 491552 | tf_op jit(solution)/shard_map/all_to_all | solution.py:313
  23.9 0.2 energy.1
  24.1 18.3 %all_to_all.19 = f32[64,1,128]{2,1,0:T(1,128)S(1)} all-to-all(f32[64,1,128]{2,1,0:T(1,128)S(1)} %bitcast.14), channel_id=1, replica_groups=mesh['pair'=4,'core'=2,'near'=4,'far'=2,'tm'=8] {'core','near','tm'}, dimensions={0} | all-to-all | bytes 65536 | tf_op jit(solution)/shard_map/all_to_all | solution.py:343
  42.4 16.4 %all_to_all.20.message_ref = f32[8,2,128]{2,1,0:T(2,128)S(1)} all-to-all(f32[8,2,128]{2,1,0:T(2,128)S(1)} %broadcast_in_dim.16), channel_id=1, replica_groups=mesh['pair'=4,'core'=2,'near'=4,'far'=2,'tm'=8] {'pair','far'}, dimensions={0} | all-to-all | bytes 16384 | tf_op jit(solution)/shard_map/all_to_all | solution.py:346
  58.8 1.2 %forces.1 = (f32[3,1000]{1,0:T(4,128)}, bf16[16,32,480]{2,1,0:T(8,128)(2,1)}) custom-call(f32[8,2,128]{2,1,0:T(2,128)S(1)} %all_to_all.20.message_ref, bf16[256,256]{1,0:T(8,128)(2,1)S(1)} %copy-done.2, bf16[256,256]{1,0:T(8,128)(2,1)S(1)} %copy-done.1, bf16[8,240,128]{2,1,0:T(8,128)(2,1)S(1)} %all-to-all-done.times_ref), custom_call_target="tpu_custom_call" | custom-call | tf_op jit(solution)/shard_map/forces/pallas_call | solution.py:348
  (3 shorter events, 0.0 us)
Async XLA Ops:
  2.8 8.5 %copy-start.3 = (f32[3,32]{1,0:T(4,128)S(1)}, f32[3,32]{1,0:T(4,128)}, u32[]{:S(2)}) copy-start(f32[3,32]{1,0:T(4,128)} %param.11) | copy-start | bytes 1156
  2.8 8.6 %copy-start = (bf16[16,32,480]{2,1,0:T(8,128)(2,1)S(1)}, bf16[16,32,480]{2,1,0:T(8,128)(2,1)}, u32[]{:S(2)}) copy-start(bf16[16,32,480]{2,1,0:T(8,128)(2,1)} %adjoint_ref.1) | copy-start | bytes 1474564
  2.8 8.6 %copy-start.1 = (bf16[256,256]{1,0:T(8,128)(2,1)S(1)}, bf16[256,256]{1,0:T(8,128)(2,1)}, u32[]{:S(2)}) copy-start(bf16[256,256]{1,0:T(8,128)(2,1)} %constant.6.clone.low_ref) | copy-start | bytes 393220
  2.8 8.6 %copy-start.2 = (bf16[256,256]{1,0:T(8,128)(2,1)S(1)}, bf16[256,256]{1,0:T(8,128)(2,1)}, u32[]{:S(2)}) copy-start(bf16[256,256]{1,0:T(8,128)(2,1)} %constant.5.clone.high_ref) | copy-start | bytes 393220
  2.8 21.1 %all-to-all-start = ((bf16[8,240,128]{2,1,0:T(8,128)(2,1)}), bf16[8,240,128]{2,1,0:T(8,128)(2,1)S(1)}, u32[]{:S(2)}, u32[]{:S(2)}) async-start(bf16[8,240,128]{2,1,0:T(8,128)(2,1)} %product.1), calls=%async_computation | async-start | bytes 983040 | tf_op jit(solution)/shard_map/all_to_all | solution.py:313

commit v9 on v6

--- a/solution.py
+++ b/solution.py
@@ -309,18 +309,18 @@
     adjoint = kernel(adjoint_kernel, "adjoint", packed, jnp.float32, 16, high, low, adjoint_w)
     message = pl.pallas_call(
         functools.partial(energy_kernel, rows),
-        out_shape=jax.ShapeDtypeStruct((CORES * n_near * n_tm, LANES), jnp.float32),
+        out_shape=jax.ShapeDtypeStruct((CORES * n_near, LANES), jnp.float32),
         compiler_params=pltpu.CompilerParams(vmem_limit_bytes=16 << 20),
         name="energy",
     )(times, adjoint, weight[None, :], label[None, :])
 
-    message = lax.all_to_all(message, ("core", "near", "tm"), split_axis=0, concat_axis=0, tiled=True)
-    message = jnp.sum(message.reshape(CORES, n_near * n_tm, LANES), axis=1)
-    message = jnp.broadcast_to(message[None], (n_pair * FAR, CORES, LANES))
-    message = lax.all_to_all(message, ("pair", "far"), split_axis=0, concat_axis=0, tiled=True)
+    message = lax.all_to_all(message, ("core", "near"), split_axis=0, concat_axis=0, tiled=True)
+    message = jnp.sum(message.reshape(CORES, n_near, LANES), axis=1)
+    message = jnp.broadcast_to(message[None], (n_pair * FAR * n_tm, CORES, LANES))
+    message = lax.all_to_all(message, ("pair", "far", "tm"), split_axis=0, concat_axis=0, tiled=True)
     shape = (NTAU, rows, width)
     forces, chi_freq = pl.pallas_call(
-        functools.partial(forces_kernel, rows, FAR),
+        functools.partial(forces_kernel, rows, FAR * n_tm),
         out_specs=[pl.BlockSpec(memory_space=pl.ANY)] * 2,
         out_shape=(
             jax.ShapeDtypeStruct((3, NATOM), jnp.float32),

time: 60.4 us -> 60.7 us (level)
  no operation moved by 1% of the time
where the time goes in v9:
time: 60.7 us; the launch traced here: 60.3 us
  blocking collectives  34.3 us (57%)
  waiting for transfers between devices  11.6 us (19%)
  starting transfers between devices  7.79 us (13%)
  Pallas kernels  4.3 us (7%)
  between operations  1.35 us (2%)
  other arithmetic  0.8 us (1%)
    all_to_all x1, blocking collectives, on_device(): lax.all_to_all(message, ('pair', 'far', 'tm'), split_axis=0, concat_axis=...  21.7 us
    all_to_all x1, blocking collectives, on_device(): lax.all_to_all(message, ('core', 'near'), split_axis=0, concat_axis=0, ti...  12.5 us
    all_to_all x1, waiting for transfers between devices, on_device(): lax.all_to_all(product, 'tm', split_axis=0, concat_axis=0, tiled=True)  11.6 us
    all_to_all x1, starting transfers between devices, on_device(): lax.all_to_all(product, 'tm', split_axis=0, concat_axis=0, tiled=True)  7.79 us
    pallas_call x1, Pallas kernels, on_device(): pl.pallas_call(product_kernel, in_specs=[pl.BlockSpec(memory_space=pl.ANY...  2.16 us
    pallas_call x1, Pallas kernels, on_device(): pl.pallas_call(functools.partial(forces_kernel, rows, FAR * n_tm), out_sp...  1.31 us
  transfers between devices with their start and end apart: 1, of which 1 were waited for; matrix products, arithmetic and copies ran while one was open for 2% of the time, Pallas kernels for 1%

profile of v9, /device:TPU:1, one launch (start us, length us, event | category | flops | bytes accessed | tf_op | source)
XLA Modules:
  0.0 60.3 jit_solution(1158436318393104529)
XLA Ops:
  0.6 2.2 %product.1 = bf16[8,240,128]{2,1,0:T(8,128)(2,1)} custom-call(bf16[2,32,3840]{2,1,0:T(8,128)(2,1)} %occ_ref.1, bf16[2,32,3840]{2,1,0:T(8,128)(2,1)} %virt_ref.1), custom_call_target="tpu_custom_call" | custom-call | tf_op jit(solution)/shard_map/product/pallas_call | solution.py:274
  2.8 0.0 copy-start.3
  2.8 0.0 copy-start
  2.8 0.0 copy-start.1
  2.8 0.0 copy-start.2
  2.8 7.8 %all-to-all-start = ((bf16[8,240,128]{2,1,0:T(8,128)(2,1)}), bf16[8,240,128]{2,1,0:T(8,128)(2,1)S(1)}, u32[]{:S(2)}, u32[]{:S(2)}) async-start(bf16[8,240,128]{2,1,0:T(8,128)(2,1)} %product.1), calls=%async_computation | async-start | bytes 983040 | tf_op jit(solution)/shard_map/all_to_all | solution.py:289
  11.3 0.0 copy-done.3
  11.3 0.1 mul.17
  11.4 0.0 copy-done
  11.4 0.0 copy-done.1
  11.4 0.0 copy-done.2
  11.4 0.6 %adjoint.1.adjoint_ref = f32[8,240,128]{2,1,0:T(8,128)S(1)} custom-call(bf16[256,256]{1,0:T(8,128)(2,1)S(1)} %copy-done.2, bf16[256,256]{1,0:T(8,128)(2,1)S(1)} %copy-done.1, bf16[16,32,480]{2,1,0:T(8,128)(2,1)S(1)} %copy-done), custom_call_target="tpu_custom_call" | custom-call | flops 251658240 | bytes 983040 | tf_op jit(solution)/shard_map/adjoint/pallas_call | solution.py:293
  12.0 0.8 %convert_multiply_fusion = f32[32]{0:T(128)S(1)} fusion(s32[30720]{0:T(1024)} %param.12, s32[]{:T(128)S(6)} %select_n.3), kind=kLoop, calls=%fused_computation.2 | loop fusion | flops 64 | bytes 260 | tf_op jit(solution)/shard_map/mul | solution.py:307
  12.8 0.1 pad_bitcast_fusion
  12.9 11.6 %all-to-all-done.times_ref = bf16[8,240,128]{2,1,0:T(8,128)(2,1)S(1)} async-done(((bf16[8,240,128]{2,1,0:T(8,128)(2,1)}), bf16[8,240,128]{2,1,0:T(8,128)(2,1)S(1)}, u32[]{:S(2)}, u32[]{:S(2)}) %all-to-all-start) | async-done | bytes 491552 | tf_op jit(solution)/shard_map/all_to_all | solution.py:289
  24.5 0.2 energy.1
  24.7 12.5 %all_to_all.19 = f32[8,1,128]{2,1,0:T(1,128)S(1)} all-to-all(f32[8,1,128]{2,1,0:T(1,128)S(1)} %bitcast.12), channel_id=1, replica_groups=mesh['pair'=4,'core'=2,'near'=4,'far'=2,'tm'=8] {'core','near'}, dimensions={0} | all-to-all | bytes 8192 | tf_op jit(solution)/shard_map/all_to_all | solution.py:317
  37.3 21.7 %all_to_all.20.message_ref = f32[64,2,128]{2,1,0:T(2,128)S(1)} all-to-all(f32[64,2,128]{2,1,0:T(2,128)S(1)} %broadcast_in_dim.16), channel_id=1, replica_groups=mesh['pair'=4,'core'=2,'near'=4,'far'=2,'tm'=8] {'pair','far','tm'}, dimensions={0} | all-to-all | bytes 131072 | tf_op jit(solution)/shard_map/all_to_all | solution.py:320
  59.0 1.3 %forces.1 = (f32[3,1000]{1,0:T(4,128)}, bf16[16,32,480]{2,1,0:T(8,128)(2,1)}) custom-call(f32[64,2,128]{2,1,0:T(2,128)S(1)} %all_to_all.20.message_ref, bf16[256,256]{1,0:T(8,128)(2,1)S(1)} %copy-done.2, bf16[256,256]{1,0:T(8,128)(2,1)S(1)} %copy-done.1, bf16[8,240,128]{2,1,0:T(8,128)(2,1)S(1)} %all-to-all-done.times_ref), custom_call_target="tpu_custom_call" | custom-call | tf_op jit(solution)/shard_map/forces/pallas_call | solution.py:322
  (3 shorter events, 0.0 us)
Async XLA Ops:
  2.8 8.5 %copy-start.3 = (f32[3,32]{1,0:T(4,128)S(1)}, f32[3,32]{1,0:T(4,128)}, u32[]{:S(2)}) copy-start(f32[3,32]{1,0:T(4,128)} %param.11) | copy-start | bytes 1156
  2.8 8.6 %copy-start = (bf16[16,32,480]{2,1,0:T(8,128)(2,1)S(1)}, bf16[16,32,480]{2,1,0:T(8,128)(2,1)}, u32[]{:S(2)}) copy-start(bf16[16,32,480]{2,1,0:T(8,128)(2,1)} %adjoint_ref.1) | copy-start | bytes 1474564
  2.8 8.6 %copy-start.1 = (bf16[256,256]{1,0:T(8,128)(2,1)S(1)}, bf16[256,256]{1,0:T(8,128)(2,1)}, u32[]{:S(2)}) copy-start(bf16[256,256]{1,0:T(8,128)(2,1)} %constant.6.clone.low_ref) | copy-start | bytes 393220
  2.8 8.6 %copy-start.2 = (bf16[256,256]{1,0:T(8,128)(2,1)S(1)}, bf16[256,256]{1,0:T(8,128)(2,1)}, u32[]{:S(2)}) copy-start(bf16[256,256]{1,0:T(8,128)(2,1)} %constant.5.clone.high_ref) | copy-start | bytes 393220
  2.8 21.7 %all-to-all-start = ((bf16[8,240,128]{2,1,0:T(8,128)(2,1)}), bf16[8,240,128]{2,1,0:T(8,128)(2,1)S(1)}, u32[]{:S(2)}, u32[]{:S(2)}) async-start(bf16[8,240,128]{2,1,0:T(8,128)(2,1)} %product.1), calls=%async_computation | async-start | bytes 983040 | tf_op jit(solution)/shard_map/all_to_all | solution.py:289
